TPU v7x, 256 devices: a whole 4x4x8 slice. The times are simulated.
256 devices in a mesh: vehicle: 4 (over y), track: 16 (over x, z_lo, core), cross: 4 (over z_hi).
Axes of the slice: x: 4, y: 4, z: 8 (z_hi: 4, z_lo: 2; z = z_hi * 2 + z_lo), core: 2. Of those that a mesh axis runs over, the one named last changes fastest.
Arguments:
- particle_offset: float32 [3, 128, 32, 128], P(None, ('vehicle', 'track'), 'cross'), may hold values from 0 to 1
- particle_velocity: float32 [3, 128, 32, 128], P(None, ('vehicle', 'track'), 'cross'), may hold values from -4 to 4
- cell_count: int32 [128, 32], P(('vehicle', 'track'), 'cross'), may hold values from 32 to 128
- face_offset: float32 [16384, 3, 128], P(('vehicle', 'track', 'cross')), may hold values from 0 to 1
- face_velocity: float32 [16384, 3, 128], P(('vehicle', 'track', 'cross')), may hold values from -4 to 4
- face_route: int32 [16384, 1], P(('vehicle', 'track', 'cross')), may hold values from 0 to 63; in each aligned block of 64 rows (0 to 63, 64 to 127, ...) at most 4 rows name the same one
- face_cell: int32 [16384], P(('vehicle', 'track', 'cross')), may hold values from 0 to 15
Outputs:
- moved_offset: float32 [3, 128, 32, 128], P(None, ('vehicle', 'track'), 'cross')
- new_velocity: float32 [3, 128, 32, 128], P(None, ('vehicle', 'track'), 'cross')
- face_impulse: float32 [16384, 3, 128], P(('vehicle', 'track', 'cross'))
Inputs may be any that keep to these rules, and one draw needn't show every extreme that they name: `face_route`: among the 64 face blocks of one owner device, at most 4 name the same terrain device, and that many is reached.
All inputs are finite; a program needn't handle non-finite values.
Results may differ from a plain program's by a relative error of at most 0.0003.
Values sent between devices are 32-bit elements; how exact they have to be, the bound alone decides.
A program may use at most 64 MiB of HBM per device.

v0:
```python
import jax
import jax.numpy as jnp
from jax import lax
from jax.sharding import PartitionSpec as P

radius = 0.1
face_radius = 0.15
stiffness = 100.0
damping = 40.0
soften = 0.05
time_step = 0.02
gravity = 9.81


def with_halo(block, sides, width):
    for axis, dim in sides:
        count = lax.axis_size(axis)
        forward = [(i, i + 1) for i in range(count - 1)]
        backward = [(target, source) for source, target in forward]
        low = lax.ppermute(
            lax.slice_in_dim(block, block.shape[dim] - width, None, axis=dim), axis, forward
        )
        high = lax.ppermute(lax.slice_in_dim(block, 0, width, axis=dim), axis, backward)
        block = jnp.concatenate([low, block, high], axis=dim)
    return block


def contact(own_pos, own_vel, other_pos, other_vel, other_live, reach):
    apart = own_pos[:, :, :, None] - other_pos[:, :, None, :]
    distance = jnp.sqrt(jnp.sum(apart * apart, axis=0) + soften * soften)
    normal = apart / distance[None]
    closing = jnp.sum((own_vel[:, :, :, None] - other_vel[:, :, None, :]) * normal, axis=0)
    intersection = jnp.maximum(reach - distance, 0.0)
    weight = intersection * (stiffness - damping * closing) * other_live[:, None, :]
    return weight[None] * normal


def particle_forces(stacked, padded):
    across = stacked.shape[2]
    slot_count = stacked.shape[3]
    others = 1.0 - jnp.eye(slot_count, dtype=jnp.float32)

    def row_force(row_index):
        own_part = lax.dynamic_slice_in_dim(stacked, row_index, 1, 1)[:, 0]
        total_force = jnp.zeros((3, across, slot_count), jnp.float32)
        for shift_t in (-1, 0, 1):
            band_rows = lax.dynamic_slice_in_dim(padded, row_index + 1 + shift_t, 1, 1)[:, 0]
            for shift_c in (-1, 0, 1):
                neighbour = band_rows[:, 1 + shift_c : 1 + shift_c + across]
                offset = jnp.array([shift_t, shift_c, 0.0], jnp.float32)[:, None, None]
                pushes = contact(
                    own_part[0:3],
                    own_part[3:6],
                    neighbour[0:3] + offset,
                    neighbour[3:6],
                    neighbour[6],
                    2.0 * radius,
                )
                if shift_t == 0 and shift_c == 0:
                    pushes = pushes * others
                total_force = total_force + jnp.sum(pushes, axis=3)
        return total_force * own_part[6][None]

    forces = lax.map(row_force, jnp.arange(stacked.shape[1], dtype=jnp.int32))
    return jnp.transpose(forces, (1, 0, 2, 3))


def tire_contact(chosen, face_pos, face_vel):
    ones_live = jnp.ones((face_pos.shape[1], face_pos.shape[2]), jnp.float32)
    pushes = contact(chosen[0:3], chosen[3:6], face_pos, face_vel, ones_live, radius + face_radius)
    pushes = pushes * chosen[6][None, :, :, None]
    return (jnp.sum(pushes, axis=3), -jnp.sum(pushes, axis=2))


def advance(offsets, velocity, stacked, face_push):
    padded = with_halo(stacked, ((("vehicle", "track"), 1), ("cross", 2)), 1)
    total_push = particle_forces(stacked, padded) + face_push
    fall = jnp.array([0.0, 0.0, -gravity], jnp.float32)[:, None, None, None]
    velocity = velocity + time_step * (total_push + fall)
    offsets = offsets + time_step * velocity
    return (offsets, velocity)


def body(
    particle_offset,
    particle_velocity,
    cell_count,
    face_offset,
    face_velocity,
    face_route,
    face_cell,
):
    travel_rows, cross_rows, slot_count = particle_offset.shape[1:]
    nblocks = travel_rows * cross_rows
    own_faces = face_offset.shape[0]
    faces = face_offset.shape[2]
    peers = lax.axis_size("track") * lax.axis_size("cross")
    capacity = max(2, 4 * own_faces // peers)
    items = peers * capacity
    live = (
        lax.broadcasted_iota(jnp.int32, (travel_rows, cross_rows, slot_count), 2)
        < cell_count[:, :, None]
    ).astype(jnp.float32)
    target = face_route[:, 0]
    first_index = lax.broadcasted_iota(jnp.int32, (own_faces, own_faces), 0)
    second_index = lax.broadcasted_iota(jnp.int32, (own_faces, own_faces), 1)
    earlier = (target[None, :] == target[:, None]) & (second_index < first_index)
    slot_index = jnp.sum(earlier.astype(jnp.int32), axis=1)
    hits = (
        lax.broadcasted_iota(jnp.int32, (own_faces, items), 1)
        == (target * capacity + slot_index)[:, None]
    )
    placement = hits.astype(jnp.float32)
    block_ids = lax.broadcasted_iota(jnp.int32, (1, nblocks), 1) + 1
    highest = lax.Precision.HIGHEST
    offsets = particle_offset
    velocity = particle_velocity
    requests = jnp.sum(hits.astype(jnp.int32) * (face_cell + 1)[:, None], axis=0)
    asked = lax.all_to_all(
        requests.reshape(peers, capacity),
        ("track", "cross"),
        split_axis=0,
        concat_axis=0,
        tiled=True,
    )
    selector = (asked.reshape(items)[:, None] == block_ids).astype(jnp.float32)
    group_size = own_faces // 4
    vel_spans = jnp.transpose(face_velocity.reshape(4, group_size, 3, faces), (0, 2, 1, 3))
    reaction = jnp.zeros((own_faces, 3, faces), jnp.float32)
    for substep in range(2):
        stacked = jnp.concatenate([offsets, velocity, live[None]], axis=0)
        chosen = jnp.einsum(
            "mk,rks->mrs", selector, stacked.reshape(7, nblocks, slot_count), precision=highest
        ).reshape(peers, capacity, 7, slot_count)
        fetched = lax.all_to_all(
            chosen, ("track", "cross"), split_axis=0, concat_axis=0, tiled=True
        )
        mine = jnp.einsum(
            "ip,prs->irs", placement, fetched.reshape(items, 7, slot_count), precision=highest
        )
        mine_spans = jnp.transpose(mine.reshape(4, group_size, 7, slot_count), (0, 2, 1, 3))
        faces_now = face_offset + substep * time_step * face_velocity
        pos_spans = jnp.transpose(faces_now.reshape(4, group_size, 3, faces), (0, 2, 1, 3))

        def owner_pass(pieces):
            return tire_contact(pieces[0], pieces[1], pieces[2])

        on_particles, on_faces = lax.map(owner_pass, (mine_spans, pos_spans, vel_spans))
        on_particles = jnp.transpose(on_particles, (0, 2, 1, 3)).reshape(own_faces, 3, slot_count)
        on_faces = jnp.transpose(on_faces, (0, 2, 1, 3)).reshape(own_faces, 3, faces)
        outgoing = jnp.einsum("ip,irs->prs", placement, on_particles, precision=highest)
        incoming = lax.all_to_all(
            outgoing.reshape(peers, capacity, 3, slot_count),
            ("track", "cross"),
            split_axis=0,
            concat_axis=0,
            tiled=True,
        )
        summed = jnp.einsum(
            "mk,mrs->rks", selector, incoming.reshape(items, 3, slot_count), precision=highest
        )
        face_push = summed.reshape(3, travel_rows, cross_rows, slot_count)
        offsets, velocity = advance(offsets, velocity, stacked, face_push)
        reaction = reaction + on_faces
    impulse = time_step * reaction
    return (offsets, velocity, impulse)


def solution(mesh):
    in_specs = (
        P(None, ("vehicle", "track"), "cross", None),
        P(None, ("vehicle", "track"), "cross", None),
        P(("vehicle", "track"), "cross"),
        P(("vehicle", "track", "cross"), None, None),
        P(("vehicle", "track", "cross"), None, None),
        P(("vehicle", "track", "cross"), None),
        P(("vehicle", "track", "cross")),
    )
    out_specs = (
        P(None, ("vehicle", "track"), "cross", None),
        P(None, ("vehicle", "track"), "cross", None),
        P(("vehicle", "track", "cross"), None, None),
    )
    return jax.shard_map(body, mesh=mesh, in_specs=in_specs, out_specs=out_specs, check_vma=False)
```

profile of v0, /device:TPU:1, one launch (start us, length us, event | category | flops | bytes accessed | tf_op | source)
XLA Modules:
  0.0 275.0 jit_solution(3737777290390571947)
XLA Ops:
  3.7 13.0 %all-to-all-start = ((s32[64,1,4]{2,1,0:T(1,128)}), s32[64,1,4]{2,1,0:T(1,128)S(1)}, u32[]{:S(2)}, u32[]{:S(2)}) async-start(s32[64,1,4]{2,1,0:T(1,128)} %bitcast.23), calls=%async_computation | async-start | bytes 65536 | tf_op jit(solution)/shard_map/all_to_all | solution.py:119
  17.5 8.3 %all-to-all-done = s32[64,1,4]{2,1,0:T(1,128)S(1)} async-done(((s32[64,1,4]{2,1,0:T(1,128)}), s32[64,1,4]{2,1,0:T(1,128)S(1)}, u32[]{:S(2)}, u32[]{:S(2)}) %all-to-all-start) | async-done | bytes 1056 | tf_op jit(solution)/shard_map/all_to_all | solution.py:119
  25.9 1.4 fusion.47
  27.3 1.5 copy.91
  28.9 5.1 %all-to-all-start.1 = ((f32[64,4,7,128]{3,1,2,0:T(4,128)}), f32[64,4,7,128]{3,1,2,0:T(4,128)S(1)}, u32[]{:S(2)}, u32[]{:S(2)}) async-start(f32[64,4,7,128]{3,1,2,0:T(4,128)} %copy.91), calls=%async_computation.1 | async-start | bytes 1835008 | tf_op jit(solution)/shard_map/all_to_all | solution.py:135
  34.1 3.6 %collective-permute-start = (f32[7,1,8,128]{3,2,0,1:T(8,128)S(1)}, f32[7,1,8,128]{3,2,0,1:T(8,128)S(1)}, u32[]{:S(2)}, u32[]{:S(2)}) collective-permute-start(f32[7,1,8,128]{3,2,0,1:T(8,128)S(1)} %copy.122), channel_id=1, source_target_pairs={{0,4},{4,8},{8,12},{12,16},{16,20},{20,24},{24,28},{28,32},{32,36}... | collective-permute-start | bytes 86024 | tf_op jit(solution)/shard_map/ppermute | solution.py:20
  37.7 1.9 collective-permute-start.1
  39.7 11.6 %collective-permute-done = f32[7,1,8,128]{3,2,0,1:T(8,128)S(1)} collective-permute-done((f32[7,1,8,128]{3,2,0,1:T(8,128)S(1)}, f32[7,1,8,128]{3,2,0,1:T(8,128)S(1)}, u32[]{:S(2)}, u32[]{:S(2)}) %collective-permute-start) | collective-permute-done | bytes 28704 | tf_op jit(solution)/shard_map/ppermute | solution.py:20
  51.4 5.6 %collective-permute-done.1 = f32[7,1,8,128]{3,2,0,1:T(8,128)S(1)} collective-permute-done((f32[7,1,8,128]{3,2,0,1:T(8,128)S(1)}, f32[7,1,8,128]{3,2,0,1:T(8,128)S(1)}, u32[]{:S(2)}, u32[]{:S(2)}) %collective-permute-start.1) | collective-permute-done | bytes 28704 | tf_op jit(solution)/shard_map/ppermute | solution.py:23
  56.9 2.8 %collective-permute-start.2 = (f32[7,4,1,128]{3,2,0,1:T(1,128)S(1)}, f32[7,4,1,128]{3,2,0,1:T(1,128)S(1)}, u32[]{:S(2)}, u32[]{:S(2)}) collective-permute-start(f32[7,4,1,128]{3,2,0,1:T(1,128)S(1)} %get-tuple-element.1010), channel_id=1, source_target_pairs={{0,1},{1,2},{2,3},{4,5},{5,6},{6,7},{8,9},{9,10},{10,11},{12,13},{... | collective-permute-start | bytes 43016 | tf_op jit(solution)/shard_map/ppermute | solution.py:20
  59.8 1.3 collective-permute-start.3
  62.5 3.9 %collective-permute-done.3 = f32[7,4,1,128]{3,2,0,1:T(1,128)S(1)} collective-permute-done((f32[7,4,1,128]{3,2,0,1:T(1,128)S(1)}, f32[7,4,1,128]{3,2,0,1:T(1,128)S(1)}, u32[]{:S(2)}, u32[]{:S(2)}) %collective-permute-start.3) | collective-permute-done | bytes 14368 | tf_op jit(solution)/shard_map/ppermute | solution.py:23
  67.1 25.4 %while.56 = (s32[]{:T(128)}, f32[4,3,16,128]{3,2,0,1:T(8,128)S(1)}, f32[4,3,16,128]{3,2,1,0:T(8,128)S(1)}, f32[4,7,16,128]{3,2,1,0:T(8,128)S(1)}, f32[4,3,16,128...) while((s32[]{:T(128)}, f32[4,3,16,128]{3,2,0,1:T(8,128)S(1)}, ...), condition=%wide.region_36.37_spmd, body=%wide.region_31.36_spmd.sunk | while | flops 12314628 | bytes 11051161 | solution.py:148
  68.5 2.0 multiply_reduce_fusion.48
  71.0 2.4 fusion.108
  73.5 1.0 fusion.107
  74.8 2.0 multiply_reduce_fusion.48
  77.3 2.4 fusion.108
  81.1 2.0 multiply_reduce_fusion.48
  83.6 2.4 fusion.108
  87.5 2.0 multiply_reduce_fusion.48
  90.0 2.4 fusion.108
  93.9 10.6 %all-to-all-start.2 = ((f32[64,4,3,128]{3,1,2,0:T(4,128)}), f32[64,4,3,128]{3,1,2,0:T(4,128)S(1)}, u32[]{:S(2)}, u32[]{:S(2)}) async-start(f32[64,4,3,128]{3,1,2,0:T(4,128)} %copy.96), calls=%async_computation.2 | async-start | bytes 786432 | tf_op jit(solution)/shard_map/all_to_all | solution.py:152
  104.7 42.7 %while.58 = (s32[]{:T(128)}, f32[2,3,8,128]{3,2,0,1:T(8,128)S(1)}, s32[2]{0:T(128)S(1)}, f32[7,2,8,128]{3,2,1,0:T(8,128)S(1)}, f32[7,4,10,128]{3,2,0,1:T(8,128)S...) while((s32[]{:T(128)}, f32[2,3,8,128]{3,2,0,1:T(8,128)S(1)}, ...), condition=%wide.region_28.29_spmd.clone.clone, body=%wide.region_0.28_spmd.sunk.clone.clone.sunk | while | flops 50012176 | bytes 48908780 | solution.py:64
  110.7 1.3 fusion.113
  112.7 2.2 multiply_reduce_fusion.50
  116.0 3.1 %multiply_reduce_fusion.51 = (f32[3,8,128]{2,1,0:T(8,128)S(1)}, f32[8,128,128]{2,1,0:T(8,128)S(1)}, f32[8,128,128]{2,1,0:T(8,128)S(1)}, f32[8,128,128]{2,1,0:T(8...) fusion(f32[8,128,128]{2,1,0:T(8,128)S(1)} %multiply_multiply_fu, ...), kind=kLoop, calls=%fused_computation.75.clone.1 | loop fusion | flops 10866688 | bytes 6516736 | tf_op jit(solution)/shard_map/while/body/eval_jaxpr/reduce_sum | solution.py:61
  119.7 1.8 multiply_reduce_fusion.52
  122.8 3.2 %multiply_reduce_fusion.53 = (f32[3,8,128]{2,1,0:T(8,128)S(1)}, f32[3,8,128]{2,1,0:T(8,128)S(1)}, f32[3,8,128]{2,1,0:T(8,128)S(1)}, f32[3,8,128]{2,1,0:T(8,128)S(1)}, f32[3,8,128]{2,1,0:T(8,128)S(1)}) fusion(f32[8,128,128]{2,1,0:T(8,128)S(1)} %multiply_multiply_fusion.42, f32[8,128,128]{2,1,0:T(8,128)S(1)} %add_sqrt_fusion.47, ...), kind=kLoop, calls=%fused_computation.77.clone.1 | loop fusion | flops 7848960 | bytes 5378048 | tf_op jit(solution)/shard_map/while/body/eval_jaxpr/reduce_sum | solution.py:61
  132.0 1.3 fusion.113
  134.1 2.2 multiply_reduce_fusion.50
  137.4 3.1 %multiply_reduce_fusion.51 = (f32[3,8,128]{2,1,0:T(8,128)S(1)}, f32[8,128,128]{2,1,0:T(8,128)S(1)}, f32[8,128,128]{2,1,0:T(8,128)S(1)}, f32[8,128,128]{2,1,0:T(8...) fusion(f32[8,128,128]{2,1,0:T(8,128)S(1)} %multiply_multiply_fu, ...), kind=kLoop, calls=%fused_computation.75.clone.1 | loop fusion | flops 10866688 | bytes 6516736 | tf_op jit(solution)/shard_map/while/body/eval_jaxpr/reduce_sum | solution.py:61
  141.1 1.8 multiply_reduce_fusion.52
  144.1 3.2 %multiply_reduce_fusion.53 = (f32[3,8,128]{2,1,0:T(8,128)S(1)}, f32[3,8,128]{2,1,0:T(8,128)S(1)}, f32[3,8,128]{2,1,0:T(8,128)S(1)}, f32[3,8,128]{2,1,0:T(8,128)S(1)}, f32[3,8,128]{2,1,0:T(8,128)S(1)}) fusion(f32[8,128,128]{2,1,0:T(8,128)S(1)} %multiply_multiply_fusion.42, f32[8,128,128]{2,1,0:T(8,128)S(1)} %add_sqrt_fusion.47, ...), kind=kLoop, calls=%fused_computation.77.clone.1 | loop fusion | flops 7848960 | bytes 5378048 | tf_op jit(solution)/shard_map/while/body/eval_jaxpr/reduce_sum | solution.py:61
  148.4 1.5 copy.100
  149.9 10.3 %all-to-all-start.3 = ((f32[64,4,7,128]{3,1,2,0:T(4,128)}), f32[64,4,7,128]{3,1,2,0:T(4,128)S(1)}, u32[]{:S(2)}, u32[]{:S(2)}) async-start(f32[64,4,7,128]{3,1,2,0:T(4,128)} %copy.100), calls=%async_computation.3 | async-start | bytes 1835008 | tf_op jit(solution)/shard_map/all_to_all | solution.py:135
  160.3 3.5 %collective-permute-start.4 = (f32[7,1,8,128]{3,2,1,0:T(8,128)S(1)}, f32[7,1,8,128]{3,2,1,0:T(8,128)S(1)}, u32[]{:S(2)}, u32[]{:S(2)}) collective-permute-start(f32[7,1,8,128]{3,2,1,0:T(8,128)S(1)} %get-tuple-element.1012), channel_id=1, source_target_pairs={{0,4},{4,8},{8,12},{12,16},{16,20},{20,24},{24,28},{28,32},{32,36}... | collective-permute-start | bytes 86024 | tf_op jit(solution)/shard_map/ppermute | solution.py:20
  163.8 1.9 collective-permute-start.5
  165.7 12.1 %collective-permute-done.4 = f32[7,1,8,128]{3,2,1,0:T(8,128)S(1)} collective-permute-done((f32[7,1,8,128]{3,2,1,0:T(8,128)S(1)}, f32[7,1,8,128]{3,2,1,0:T(8,128)S(1)}, u32[]{:S(2)}, u32[]{:S(2)}) %collective-permute-start.4) | collective-permute-done | bytes 28704 | tf_op jit(solution)/shard_map/ppermute | solution.py:20
  177.8 5.3 %collective-permute-done.5 = f32[7,1,8,128]{3,2,1,0:T(8,128)S(1)} collective-permute-done((f32[7,1,8,128]{3,2,1,0:T(8,128)S(1)}, f32[7,1,8,128]{3,2,1,0:T(8,128)S(1)}, u32[]{:S(2)}, u32[]{:S(2)}) %collective-permute-start.5) | collective-permute-done | bytes 28704 | tf_op jit(solution)/shard_map/ppermute | solution.py:23
  183.2 2.8 %collective-permute-start.6 = (f32[7,4,1,128]{3,2,1,0:T(1,128)S(1)}, f32[7,4,1,128]{3,2,1,0:T(1,128)S(1)}, u32[]{:S(2)}, u32[]{:S(2)}) collective-permute-start(f32[7,4,1,128]{3,2,1,0:T(1,128)S(1)} %get-tuple-element.1008), channel_id=1, source_target_pairs={{0,1},{1,2},{2,3},{4,5},{5,6},{6,7},{8,9},{9,10},{10,11},{12,13},{... | collective-permute-start | bytes 43016 | tf_op jit(solution)/shard_map/ppermute | solution.py:20
  186.0 1.5 collective-permute-start.7
  187.5 5.1 %collective-permute-done.7 = f32[7,4,1,128]{3,2,1,0:T(1,128)S(1)} collective-permute-done((f32[7,4,1,128]{3,2,1,0:T(1,128)S(1)}, f32[7,4,1,128]{3,2,1,0:T(1,128)S(1)}, u32[]{:S(2)}, u32[]{:S(2)}) %collective-permute-start.7) | collective-permute-done | bytes 14368 | tf_op jit(solution)/shard_map/ppermute | solution.py:23
  193.3 25.4 %while.57 = (s32[]{:T(128)}, f32[4,3,16,128]{3,2,0,1:T(8,128)S(1)}, f32[4,3,16,128]{3,2,1,0:T(8,128)S(1)}, f32[4,7,16,128]{3,2,1,0:T(8,128)S(1)}, f32[4,3,16,128...) while((s32[]{:T(128)}, f32[4,3,16,128]{3,2,0,1:T(8,128)S(1)}, ...), condition=%wide.region_71.72_spmd, body=%wide.region_66.0_spmd.sunk | while | flops 12314628 | bytes 11051161 | solution.py:148
  194.7 2.0 multiply_reduce_fusion.49
  197.2 2.4 fusion.110
  201.0 2.0 multiply_reduce_fusion.49
  203.5 2.4 fusion.110
  207.4 2.0 multiply_reduce_fusion.49
  209.9 2.4 fusion.110
  213.7 2.0 multiply_reduce_fusion.49
  216.2 2.4 fusion.110
  220.0 10.5 %all-to-all-start.4 = ((f32[64,4,3,128]{3,1,2,0:T(4,128)}), f32[64,4,3,128]{3,1,2,0:T(4,128)S(1)}, u32[]{:S(2)}, u32[]{:S(2)}) async-start(f32[64,4,3,128]{3,1,2,0:T(4,128)} %copy.105), calls=%async_computation.4 | async-start | bytes 786432 | tf_op jit(solution)/shard_map/all_to_all | solution.py:152
  230.6 42.7 %while.59 = (s32[]{:T(128)}, f32[2,3,8,128]{3,2,0,1:T(8,128)S(1)}, s32[2]{0:T(128)S(1)}, f32[7,2,8,128]{3,2,1,0:T(8,128)S(1)}, f32[7,4,10,128]{3,2,0,1:T(8,128)S...) while((s32[]{:T(128)}, f32[2,3,8,128]{3,2,0,1:T(8,128)S(1)}, ...), condition=%wide.region_65.66_spmd.clone.clone, body=%wide.region_37.65_spmd.sunk.clone.clone.sunk | while | flops 50012176 | bytes 48908780 | solution.py:64
  236.6 1.3 fusion.116
  238.6 2.2 multiply_reduce_fusion.54
  241.9 3.1 %multiply_reduce_fusion.55 = (f32[3,8,128]{2,1,0:T(8,128)S(1)}, f32[8,128,128]{2,1,0:T(8,128)S(1)}, f32[8,128,128]{2,1,0:T(8,128)S(1)}, f32[8,128,128]{2,1,0:T(8...) fusion(f32[8,128,128]{2,1,0:T(8,128)S(1)} %multiply_multiply_fu, ...), kind=kLoop, calls=%fused_computation.165.clone.1 | loop fusion | flops 10866688 | bytes 6516736 | tf_op jit(solution)/shard_map/while/body/eval_jaxpr/reduce_sum | solution.py:61
  245.7 1.8 multiply_reduce_fusion.56
  248.7 3.2 %multiply_reduce_fusion.57 = (f32[3,8,128]{2,1,0:T(8,128)S(1)}, f32[3,8,128]{2,1,0:T(8,128)S(1)}, f32[3,8,128]{2,1,0:T(8,128)S(1)}, f32[3,8,128]{2,1,0:T(8,128)S(1)}, f32[3,8,128]{2,1,0:T(8,128)S(1)}) fusion(f32[8,128,128]{2,1,0:T(8,128)S(1)} %multiply_multiply_fusion.51, f32[8,128,128]{2,1,0:T(8,128)S(1)} %add_sqrt_fusion.56, ...), kind=kLoop, calls=%fused_computation.167.clone.1 | loop fusion | flops 7848960 | bytes 5378048 | tf_op jit(solution)/shard_map/while/body/eval_jaxpr/reduce_sum | solution.py:61
  258.0 1.3 fusion.116
  260.0 2.2 multiply_reduce_fusion.54
  263.3 3.1 %multiply_reduce_fusion.55 = (f32[3,8,128]{2,1,0:T(8,128)S(1)}, f32[8,128,128]{2,1,0:T(8,128)S(1)}, f32[8,128,128]{2,1,0:T(8,128)S(1)}, f32[8,128,128]{2,1,0:T(8...) fusion(f32[8,128,128]{2,1,0:T(8,128)S(1)} %multiply_multiply_fu, ...), kind=kLoop, calls=%fused_computation.165.clone.1 | loop fusion | flops 10866688 | bytes 6516736 | tf_op jit(solution)/shard_map/while/body/eval_jaxpr/reduce_sum | solution.py:61
  267.0 1.8 multiply_reduce_fusion.56
  270.1 3.2 %multiply_reduce_fusion.57 = (f32[3,8,128]{2,1,0:T(8,128)S(1)}, f32[3,8,128]{2,1,0:T(8,128)S(1)}, f32[3,8,128]{2,1,0:T(8,128)S(1)}, f32[3,8,128]{2,1,0:T(8,128)S(1)}, f32[3,8,128]{2,1,0:T(8,128)S(1)}) fusion(f32[8,128,128]{2,1,0:T(8,128)S(1)} %multiply_multiply_fusion.51, f32[8,128,128]{2,1,0:T(8,128)S(1)} %add_sqrt_fusion.56, ...), kind=kLoop, calls=%fused_computation.167.clone.1 | loop fusion | flops 7848960 | bytes 5378048 | tf_op jit(solution)/shard_map/while/body/eval_jaxpr/reduce_sum | solution.py:61
  (267 shorter events, 43.3 us)
Async XLA Ops:
  3.7 22.2 %all-to-all-start = ((s32[64,1,4]{2,1,0:T(1,128)}), s32[64,1,4]{2,1,0:T(1,128)S(1)}, u32[]{:S(2)}, u32[]{:S(2)}) async-start(s32[64,1,4]{2,1,0:T(1,128)} %bitcast.23), calls=%async_computation | async-start | bytes 65536 | tf_op jit(solution)/shard_map/all_to_all | solution.py:119
  28.8 5.1 %copy-start.15 = (s32[2,8]{1,0:T(2,128)S(1)}, s32[2,8]{1,0:T(2,128)}, u32[]{:S(2)}) copy-start(s32[2,8]{1,0:T(2,128)} %param.37) | copy-start | bytes 196
  28.8 5.2 %copy-start = (f32[3,2,8,128]{3,2,1,0:T(8,128)S(1)}, f32[3,2,8,128]{3,2,1,0:T(8,128)}, u32[]{:S(2)}) copy-start(f32[3,2,8,128]{3,2,1,0:T(8,128)} %param.35) | copy-start | bytes 73732
  28.8 5.2 %copy-start.1 = (f32[3,2,8,128]{3,2,1,0:T(8,128)S(1)}, f32[3,2,8,128]{3,2,1,0:T(8,128)}, u32[]{:S(2)}) copy-start(f32[3,2,8,128]{3,2,1,0:T(8,128)} %param.36) | copy-start | bytes 73732
  28.8 10.8 %copy-start.2 = (f32[64,3,128]{2,0,1:T(8,128)S(1)}, f32[64,3,128]{2,0,1:T(8,128)}, u32[]{:S(2)}) copy-start(f32[64,3,128]{2,0,1:T(8,128)} %param.39) | copy-start | bytes 294916
  28.9 10.8 %copy-start.5 = (f32[64,3,128]{2,0,1:T(8,128)S(1)}, f32[64,3,128]{2,0,1:T(8,128)}, u32[]{:S(2)}) copy-start(f32[64,3,128]{2,0,1:T(8,128)} %param.38) | copy-start | bytes 294916
  28.9 37.5 %all-to-all-start.1 = ((f32[64,4,7,128]{3,1,2,0:T(4,128)}), f32[64,4,7,128]{3,1,2,0:T(4,128)S(1)}, u32[]{:S(2)}, u32[]{:S(2)}) async-start(f32[64,4,7,128]{3,1,2,0:T(4,128)} %copy.91), calls=%async_computation.1 | async-start | bytes 1835008 | tf_op jit(solution)/shard_map/all_to_all | solution.py:135
  34.1 17.2 %collective-permute-start = (f32[7,1,8,128]{3,2,0,1:T(8,128)S(1)}, f32[7,1,8,128]{3,2,0,1:T(8,128)S(1)}, u32[]{:S(2)}, u32[]{:S(2)}) collective-permute-start(f32[7,1,8,128]{3,2,0,1:T(8,128)S(1)} %copy.122), channel_id=1, source_target_pairs={{0,4},{4,8},{8,12},{12,16},{16,20},{20,24},{24,28},{28,32},{32,36}... | collective-permute-start | bytes 86024 | tf_op jit(solution)/shard_map/ppermute | solution.py:20
  37.7 19.2 %collective-permute-start.1 = (f32[7,1,8,128]{3,2,0,1:T(8,128)S(1)}, f32[7,1,8,128]{3,2,0,1:T(8,128)S(1)}, u32[]{:S(2)}, u32[]{:S(2)}) collective-permute-start(f32[7,1,8,128]{3,2,0,1:T(8,128)S(1)} %copy.123), channel_id=1, source_target_pairs={{4,0},{8,4},{12,8},{16,12},{20,16},{24,20},{28,24},{32,28},{36,32}... | collective-permute-start | bytes 86024 | tf_op jit(solution)/shard_map/ppermute | solution.py:23
  56.9 5.5 %collective-permute-start.2 = (f32[7,4,1,128]{3,2,0,1:T(1,128)S(1)}, f32[7,4,1,128]{3,2,0,1:T(1,128)S(1)}, u32[]{:S(2)}, u32[]{:S(2)}) collective-permute-start(f32[7,4,1,128]{3,2,0,1:T(1,128)S(1)} %get-tuple-element.1010), channel_id=1, source_target_pairs={{0,1},{1,2},{2,3},{4,5},{5,6},{6,7},{8,9},{9,10},{10,11},{12,13},{... | collective-permute-start | bytes 43016 | tf_op jit(solution)/shard_map/ppermute | solution.py:20
  59.8 6.6 %collective-permute-start.3 = (f32[7,4,1,128]{3,2,0,1:T(1,128)S(1)}, f32[7,4,1,128]{3,2,0,1:T(1,128)S(1)}, u32[]{:S(2)}, u32[]{:S(2)}) collective-permute-start(f32[7,4,1,128]{3,2,0,1:T(1,128)S(1)} %get-tuple-element.1011), channel_id=1, source_target_pairs={{1,0},{2,1},{3,2},{5,4},{6,5},{7,6},{9,8},{10,9},{11,10},{13,12},{... | collective-permute-start | bytes 43016 | tf_op jit(solution)/shard_map/ppermute | solution.py:23
  92.4 12.1 %copy-start.3 = (f32[4,3,16,128]{3,2,1,0:T(8,128)}, f32[4,3,16,128]{3,2,1,0:T(8,128)S(1)}, u32[]{:S(2)}) copy-start(f32[4,3,16,128]{3,2,1,0:T(8,128)S(1)} %get-tuple-element.663) | copy-start | bytes 294916
  92.5 12.1 %copy-start.6 = (f32[3]{0:T(128)S(1)}, f32[3]{0:T(128)}, u32[]{:S(2)}) copy-start(f32[3]{0:T(128)} %constant.274.clone..sunk.6) | copy-start | bytes 40
  92.5 12.1 %copy-start.7 = (f32[3]{0:T(128)S(1)}, f32[3]{0:T(128)}, u32[]{:S(2)}) copy-start(f32[3]{0:T(128)} %constant.275.clone..sunk.6) | copy-start | bytes 40
  92.5 12.1 %copy-start.8 = (f32[3]{0:T(128)S(1)}, f32[3]{0:T(128)}, u32[]{:S(2)}) copy-start(f32[3]{0:T(128)} %constant.276.clone..sunk.6) | copy-start | bytes 40
  92.5 12.1 %copy-start.9 = (f32[3]{0:T(128)S(1)}, f32[3]{0:T(128)}, u32[]{:S(2)}) copy-start(f32[3]{0:T(128)} %constant.277.clone..sunk.6) | copy-start | bytes 40
  92.5 12.1 %copy-start.10 = (f32[3]{0:T(128)S(1)}, f32[3]{0:T(128)}, u32[]{:S(2)}) copy-start(f32[3]{0:T(128)} %constant.279.clone..sunk.6) | copy-start | bytes 40
  92.5 12.1 %copy-start.11 = (f32[3]{0:T(128)S(1)}, f32[3]{0:T(128)}, u32[]{:S(2)}) copy-start(f32[3]{0:T(128)} %constant.280.clone..sunk.6) | copy-start | bytes 40
  92.5 12.1 %copy-start.12 = (f32[3]{0:T(128)S(1)}, f32[3]{0:T(128)}, u32[]{:S(2)}) copy-start(f32[3]{0:T(128)} %constant.281.clone..sunk.6) | copy-start | bytes 40
  92.5 12.1 %copy-start.13 = (f32[3]{0:T(128)S(1)}, f32[3]{0:T(128)}, u32[]{:S(2)}) copy-start(f32[3]{0:T(128)} %constant.282.clone..sunk.6) | copy-start | bytes 40
  93.9 53.5 %all-to-all-start.2 = ((f32[64,4,3,128]{3,1,2,0:T(4,128)}), f32[64,4,3,128]{3,1,2,0:T(4,128)S(1)}, u32[]{:S(2)}, u32[]{:S(2)}) async-start(f32[64,4,3,128]{3,1,2,0:T(4,128)} %copy.96), calls=%async_computation.2 | async-start | bytes 786432 | tf_op jit(solution)/shard_map/all_to_all | solution.py:152
  104.6 42.9 %copy-start.14 = (f32[3]{0:T(128)S(1)}, f32[3]{0:T(128)}, u32[]{:S(2)}) copy-start(f32[3]{0:T(128)} %constant.283.clone) | copy-start | bytes 40
  149.9 42.7 %all-to-all-start.3 = ((f32[64,4,7,128]{3,1,2,0:T(4,128)}), f32[64,4,7,128]{3,1,2,0:T(4,128)S(1)}, u32[]{:S(2)}, u32[]{:S(2)}) async-start(f32[64,4,7,128]{3,1,2,0:T(4,128)} %copy.100), calls=%async_computation.3 | async-start | bytes 1835008 | tf_op jit(solution)/shard_map/all_to_all | solution.py:135
  160.3 17.6 %collective-permute-start.4 = (f32[7,1,8,128]{3,2,1,0:T(8,128)S(1)}, f32[7,1,8,128]{3,2,1,0:T(8,128)S(1)}, u32[]{:S(2)}, u32[]{:S(2)}) collective-permute-start(f32[7,1,8,128]{3,2,1,0:T(8,128)S(1)} %get-tuple-element.1012), channel_id=1, source_target_pairs={{0,4},{4,8},{8,12},{12,16},{16,20},{20,24},{24,28},{28,32},{32,36}... | collective-permute-start | bytes 86024 | tf_op jit(solution)/shard_map/ppermute | solution.py:20
  163.8 19.3 %collective-permute-start.5 = (f32[7,1,8,128]{3,2,1,0:T(8,128)S(1)}, f32[7,1,8,128]{3,2,1,0:T(8,128)S(1)}, u32[]{:S(2)}, u32[]{:S(2)}) collective-permute-start(f32[7,1,8,128]{3,2,1,0:T(8,128)S(1)} %get-tuple-element.1013), channel_id=1, source_target_pairs={{4,0},{8,4},{12,8},{16,12},{20,16},{24,20},{28,24},{32,28},{36,32}... | collective-permute-start | bytes 86024 | tf_op jit(solution)/shard_map/ppermute | solution.py:23
  183.2 4.3 %collective-permute-start.6 = (f32[7,4,1,128]{3,2,1,0:T(1,128)S(1)}, f32[7,4,1,128]{3,2,1,0:T(1,128)S(1)}, u32[]{:S(2)}, u32[]{:S(2)}) collective-permute-start(f32[7,4,1,128]{3,2,1,0:T(1,128)S(1)} %get-tuple-element.1008), channel_id=1, source_target_pairs={{0,1},{1,2},{2,3},{4,5},{5,6},{6,7},{8,9},{9,10},{10,11},{12,13},{... | collective-permute-start | bytes 43016 | tf_op jit(solution)/shard_map/ppermute | solution.py:20
  186.0 6.6 %collective-permute-start.7 = (f32[7,4,1,128]{3,2,1,0:T(1,128)S(1)}, f32[7,4,1,128]{3,2,1,0:T(1,128)S(1)}, u32[]{:S(2)}, u32[]{:S(2)}) collective-permute-start(f32[7,4,1,128]{3,2,1,0:T(1,128)S(1)} %get-tuple-element.1009), channel_id=1, source_target_pairs={{1,0},{2,1},{3,2},{5,4},{6,5},{7,6},{9,8},{10,9},{11,10},{13,12},{... | collective-permute-start | bytes 43016 | tf_op jit(solution)/shard_map/ppermute | solution.py:23
  220.0 54.0 %all-to-all-start.4 = ((f32[64,4,3,128]{3,1,2,0:T(4,128)}), f32[64,4,3,128]{3,1,2,0:T(4,128)S(1)}, u32[]{:S(2)}, u32[]{:S(2)}) async-start(f32[64,4,3,128]{3,1,2,0:T(4,128)} %copy.105), calls=%async_computation.4 | async-start | bytes 786432 | tf_op jit(solution)/shard_map/all_to_all | solution.py:152
  230.6 42.8 %copy-start.4 = (f32[4,3,16,128]{3,2,1,0:T(8,128)S(1)}, f32[4,3,16,128]{3,2,1,0:T(8,128)}, u32[]{:S(2)}) copy-start(f32[4,3,16,128]{3,2,1,0:T(8,128)} %copy-done.3) | copy-start | bytes 294916
where the time goes:
time: 276 us; the launch traced here: 275 us
  other arithmetic  114 us (41%)
  starting transfers between devices  68.9 us (25%)
  waiting for transfers between devices  51.8 us (19%)
  loops' own time  22.3 us (8%)
  local copies, waits for them, and re-layouts  11.5 us (4%)
  matrix products  4.84 us (2%)
    reduce_sum x16, other arithmetic, contact(): jnp.sum((own_vel[:, :, :, None] - other_vel[:, :, None, :]) * normal, axi...  32.2 us
    reduce_sum x8, other arithmetic, row_force(): total_force = total_force + jnp.sum(pushes, axis=3)  25.4 us
    ppermute x4, waiting for transfers between devices, with_halo(): lax.ppermute(lax.slice_in_dim(block, block.shape[dim] - width, None, axis...  23.7 us
    another operation x2, loops' own time, particle_forces(): forces = lax.map(row_force, jnp.arange(stacked.shape[1], dtype=jnp.int32))  21.6 us
    all_to_all x2, starting transfers between devices, body(): lax.all_to_all(outgoing.reshape(peers, capacity, 3, slot_count), ('track'...  21.1 us
    ppermute x4, waiting for transfers between devices, with_halo(): lax.ppermute(lax.slice_in_dim(block, 0, width, axis=dim), axis, backward)  19.8 us
    reduce_sum x8, other arithmetic, tire_contact(): return (jnp.sum(pushes, axis=3), -jnp.sum(pushes, axis=2))  19.3 us
    all_to_all x2, starting transfers between devices, body(): lax.all_to_all(chosen, ('track', 'cross'), split_axis=0, concat_axis=0, t...  15.4 us
  transfers between devices with their start and end apart: 13, of which 7 were waited for; matrix products, arithmetic and copies ran while one was open for 24% of the time, Pallas kernels for 0%

commit v1 on v0

v1 whole, which is shorter than its diff:
```python
import functools

import jax
import jax.numpy as jnp
from jax import lax
from jax.experimental import pallas as pl
from jax.experimental.pallas import tpu as pltpu
from jax.sharding import PartitionSpec as P

radius = 0.1
face_radius = 0.15
stiffness = 100.0
damping = 40.0
soften = 0.05
time_step = 0.02
gravity = 9.81
away = 1.0e6

F32 = jnp.float32
MESH = pl.DeviceIdType.MESH
VM = pl.BlockSpec(memory_space=pltpu.VMEM)
SM = pl.BlockSpec(memory_space=pltpu.SMEM)
SIDES = [(a, b) for a in (-1, 0, 1) for b in (-1, 0, 1) if (a, b) != (0, 0)]
N_PEERS = 64


def rows():
    return lax.broadcasted_iota(jnp.int32, (8, 128), 0)


def lanes():
    return lax.broadcasted_iota(jnp.int32, (8, 128), 1)


def roll(tile, shift):
    return pltpu.roll(tile, shift, axis=0)


def resting(sign):
    return jnp.where(rows() == 2, sign * away, 0.0)


def scaled(tile):
    row = rows()
    return jnp.where(row < 3, tile, jnp.where(row < 6, -damping * tile, 0.0))


def spread(tile):
    return [jnp.broadcast_to(tile[channel : channel + 1], (8, 128)) for channel in range(6)]


def pushes(own, other, reach):
    x, y, z = (own[axis] - other[axis] for axis in range(3))
    square = x * x + (y * y + (z * z + soften * soften))
    inverse = lax.rsqrt(square)
    depth = jnp.maximum(reach - square * inverse, 0.0) * inverse
    closing = (own[3] - other[3]) * x + (own[4] - other[4]) * y + (own[5] - other[5]) * z
    weight = depth * (stiffness + closing * inverse)
    return weight * x, weight * y, weight * z


def across_lanes(sums_ref, cell):
    found = [jnp.sum(sums_ref[cell, axis].T, axis=0, keepdims=True) for axis in range(3)]
    return jnp.concatenate(found + [jnp.zeros((5, 128), F32)], axis=0)


def place():
    track = lax.axis_index("track")
    cross = lax.axis_index("cross")
    return lax.axis_index("vehicle"), track, cross


def peer_at(step, sign):
    _, track, cross = place()
    dz, dx, dc = step % 8, (step // 8) % 4, step // 32
    x = (track // 4 + 4 + sign * dx) % 4
    z = (cross * 2 + (track // 2) % 2 + 8 + sign * dz) % 8
    core = (track % 2 + dc) % 2
    return x * 4 + (z % 2) * 2 + core, z // 2


def neighbour(side):
    vehicle, track, cross = place()
    row = (vehicle * 16 + track + 64 + side[0]) % 64
    return row // 16, row % 16, (cross + 4 + side[1]) % 4


def greet():
    vehicle = lax.axis_index("vehicle")
    barrier = pltpu.get_barrier_semaphore()

    def one(step, carry):
        track, cross = peer_at(step, 1)
        pl.semaphore_signal(
            barrier, inc=1, device_id=(vehicle, track, cross), device_id_type=MESH
        )
        return carry

    for side in SIDES:
        pl.semaphore_signal(barrier, inc=1, device_id=neighbour(side), device_id_type=MESH)
    lax.fori_loop(1, N_PEERS, one, 0)
    pl.semaphore_wait(barrier, N_PEERS - 1 + len(SIDES))


def halo_copy(index, ring, send_sem, recv_sem):
    down, right = SIDES[index]
    source_row = {1: pl.ds(2, 1), -1: pl.ds(1, 1), 0: pl.ds(1, 2)}[down]
    target_row = {1: pl.ds(0, 1), -1: pl.ds(3, 1), 0: pl.ds(1, 2)}[down]
    source_column = {1: pl.ds(8, 1), -1: pl.ds(1, 1), 0: pl.ds(1, 8)}[right]
    target_column = {1: pl.ds(0, 1), -1: pl.ds(9, 1), 0: pl.ds(1, 8)}[right]
    return pltpu.make_async_remote_copy(
        src_ref=ring.at[source_row, source_column],
        dst_ref=ring.at[target_row, target_column],
        send_sem=send_sem.at[index],
        recv_sem=recv_sem.at[index],
        device_id=neighbour(SIDES[index]),
        device_id_type=MESH,
    )


def block_copy(step, outgoing, incoming, send_sem, recv_sem):
    vehicle, track, cross = place()
    to_track, to_cross = peer_at(step, 1)
    return pltpu.make_async_remote_copy(
        src_ref=outgoing.at[to_track * 4 + to_cross],
        dst_ref=incoming.at[track * 4 + cross],
        send_sem=send_sem.at[step],
        recv_sem=recv_sem.at[step],
        device_id=(vehicle, to_track, to_cross),
        device_id_type=MESH,
    )


def order(turn):
    return (turn * 21) % 64


def set_up_cells(state_ref, count_ref, columns_ref, ring_ref=None):
    def one(cell, carry):
        alive = lanes() < count_ref[cell // 8, cell % 8]
        tile = scaled(state_ref[cell])
        own = jnp.where(alive, tile, resting(1.0))
        for channel in range(6):
            line = jnp.broadcast_to(own[channel : channel + 1], (128, 128))
            columns_ref[cell, channel] = line.T
        if ring_ref is not None:
            ring_ref[cell // 8 + 1, cell % 8 + 1] = jnp.where(alive, tile, resting(-1.0))
        return carry

    lax.fori_loop(0, 16, one, 0)


def clear_edges(ring_ref):
    vehicle, track, cross = place()
    line = vehicle * 16 + track
    dead = resting(-1.0)

    @pl.when(line == 0)
    def _():
        for column in range(10):
            ring_ref[0, column] = dead

    @pl.when(line == 63)
    def _():
        for column in range(10):
            ring_ref[3, column] = dead

    @pl.when(cross == 0)
    def _():
        for row in range(4):
            ring_ref[row, 0] = dead

    @pl.when(cross == 3)
    def _():
        for row in range(4):
            ring_ref[row, 9] = dead


def particle_pushes(ring_ref, columns_ref, sums_ref, out_ref):
    width = 2

    def one(turn, carry):
        cell = turn // (16 // width)
        row_index, column = cell // 8, cell % 8
        for part in range(width):
            start = pl.multiple_of((turn % (16 // width)) * (8 * width) + 8 * part, 8)
            own = [columns_ref[cell, channel, pl.ds(start, 8), :] for channel in range(6)]
            total = [0.0, 0.0, 0.0]
            for down in (-1, 0, 1):
                for right in (-1, 0, 1):
                    other = spread(ring_ref[row_index + 1 + down, column + 1 + right])
                    shifted = [own[0] - float(down), own[1] - float(right)] + own[2:]
                    push = pushes(shifted, other, 2.0 * radius)
                    total = [total[axis] + push[axis] for axis in range(3)]
            for axis in range(3):
                sums_ref[cell, axis, pl.ds(start, 8), :] = total[axis]
        return carry

    lax.fori_loop(0, 256 // width, one, 0)

    def gather(cell, carry):
        out_ref[cell] = across_lanes(sums_ref, cell)
        return carry

    lax.fori_loop(0, 16, gather, 0)


def pack_kernel(po_ref, pv_ref, fo_ref, fv_ref, route_ref, cell_ref, state_ref, send_ref, meta_ref, pos_ref, used):
    for row in range(2):
        for column in range(8):
            cell = row * 8 + column
            for channel in range(3):
                state_ref[cell, channel : channel + 1, :] = po_ref[channel, row, column : column + 1, :]
                state_ref[cell, channel + 3 : channel + 4, :] = pv_ref[channel, row, column : column + 1, :]
            state_ref[cell, 6:8, :] = jnp.zeros((2, 128), F32)
    meta_ref[...] = jnp.full(meta_ref.shape, -1, jnp.int32)

    def clear(index, carry):
        used[index] = 0
        return carry

    lax.fori_loop(0, N_PEERS, clear, 0)
    lane = lax.broadcasted_iota(jnp.int32, (1, 128), 1)

    def one(block, carry):
        target = route_ref[block, 0]
        slot = used[target]
        used[target] = slot + 1
        pos_ref[block] = target * 4 + slot
        meta_ref[target] = jnp.where(lane == slot, cell_ref[block], meta_ref[target])
        for channel in range(3):
            send_ref[target, pl.ds(slot * 6 + channel, 1), :] = fo_ref[block, channel : channel + 1, :]
            send_ref[target, pl.ds(slot * 6 + 3 + channel, 1), :] = fv_ref[block, channel : channel + 1, :]
        return carry

    lax.fori_loop(0, N_PEERS, one, 0)


def first_kernel(
    state_ref, send_ref, meta_ref, count_ref,
    faces_ref, cells_ref, push_ref,
    recv, recv_meta, ring, columns, sums,
    data_out, data_in, meta_out, meta_in, halo_out, halo_in,
):
    _, track, cross = place()
    me = track * 4 + cross
    set_up_cells(state_ref, count_ref, columns, ring)
    greet()
    for index in range(8):
        halo_copy(index, ring, halo_out, halo_in).start()

    def start(turn, carry):
        step = order(turn)
        block_copy(step, meta_ref, recv_meta, meta_out, meta_in).start()
        block_copy(step, send_ref, recv, data_out, data_in).start()
        return carry

    lax.fori_loop(1, N_PEERS, start, 0)
    for index in range(8):
        halo_copy(index, ring, halo_out, halo_in).wait()
    clear_edges(ring)
    particle_pushes(ring, columns, sums, push_ref)
    for slot in range(4):
        faces_ref[me * 4 + slot, 0:6, :] = send_ref[me, slot * 6 : slot * 6 + 6, :]
    cells_ref[me] = meta_ref[me]

    def finish(turn, carry):
        step = order(turn)
        block_copy(step, meta_ref, recv_meta, meta_out, meta_in).wait()
        block_copy(step, send_ref, recv, data_out, data_in).wait()
        from_track, from_cross = peer_at(step, -1)
        source = from_track * 4 + from_cross
        for slot in range(4):
            faces_ref[source * 4 + slot, 0:6, :] = recv[source, slot * 6 : slot * 6 + 6, :]
        cells_ref[source] = recv_meta[source]
        return carry

    lax.fori_loop(1, N_PEERS, finish, 0)


def face_kernel(
    faces_ref, cells_ref, state_ref, push_ref, count_ref,
    next_ref, later_ref, impulse_ref,
    columns, sums, total, reaction, listing,
):
    def gather(index, found):
        listing[found] = index
        return found + (cells_ref[index // 4, 0, index % 4] >= 0).astype(jnp.int32)

    found = lax.fori_loop(0, 256, gather, 0, unroll=8)

    def sweep(second_step):
        sums[...] = jnp.zeros_like(sums)

        def one(turn, carry):
            slot = listing[turn]
            cell = cells_ref[slot // 4, 0, slot % 4]
            tile = faces_ref[slot]
            row = rows()
            tile = jnp.where(row < 6, tile, 0.0)
            if second_step:
                tile = tile + jnp.where(row < 3, time_step * roll(tile, 5), 0.0)
            other = spread(scaled(tile))
            spans = (count_ref[cell // 8, cell % 8] + 31) // 32

            def meet(count):
                back = [0.0, 0.0, 0.0]
                for part in range(count):
                    span = slice(8 * part, 8 * part + 8)
                    own = [columns[cell, channel, span, :] for channel in range(6)]
                    push = pushes(own, other, radius + face_radius)
                    for axis in range(3):
                        sums[cell, axis, span, :] = sums[cell, axis, span, :] + push[axis]
                        back[axis] = back[axis] + push[axis]
                for axis in range(3):
                    line = -time_step * jnp.sum(back[axis], axis=0, keepdims=True)
                    if second_step:
                        impulse_ref[slot, axis : axis + 1, :] = reaction[slot, axis : axis + 1, :] + line
                    else:
                        reaction[slot, axis : axis + 1, :] = line

            for number in range(1, 5):
                pl.when(spans == number)(functools.partial(meet, 4 * number))
            return carry

        lax.fori_loop(0, found, one, 0)

        def collect(cell, carry):
            total[cell] = across_lanes(sums, cell)
            return carry

        lax.fori_loop(0, 16, collect, 0)

    set_up_cells(state_ref, count_ref, columns)
    sweep(False)

    def advance(cell, carry):
        next_ref[cell] = advanced(
            state_ref[cell], push_ref[cell] + total[cell], count_ref[cell // 8, cell % 8]
        )
        return carry

    lax.fori_loop(0, 16, advance, 0)
    set_up_cells(next_ref, count_ref, columns)
    sweep(True)
    later_ref[...] = total[...]


def advanced(tile, push, count):
    row = rows()
    force = jnp.where((row < 3) & (lanes() < count), push, 0.0)
    force = force + jnp.where(row == 2, -gravity, 0.0)
    tile = tile + jnp.where((row >= 3) & (row < 6), time_step * roll(force, 3), 0.0)
    return tile + jnp.where(row < 3, time_step * roll(tile, 5), 0.0)


def second_kernel(
    state_ref, impulse_ref, count_ref,
    push_ref, back_ref,
    outgoing, recv, ring, columns, sums,
    data_out, data_in, halo_out, halo_in,
):
    _, track, cross = place()
    me = track * 4 + cross
    set_up_cells(state_ref, count_ref, columns, ring)
    greet()
    for index in range(8):
        halo_copy(index, ring, halo_out, halo_in).start()

    def start(turn, carry):
        step = order(turn)
        to_track, to_cross = peer_at(step, 1)
        target = to_track * 4 + to_cross
        for slot in range(4):
            outgoing[target, slot * 3 : slot * 3 + 3, :] = impulse_ref[target * 4 + slot, 0:3, :]
        block_copy(step, outgoing, recv, data_out, data_in).start()
        return carry

    lax.fori_loop(1, N_PEERS, start, 0)
    for index in range(8):
        halo_copy(index, ring, halo_out, halo_in).wait()
    clear_edges(ring)
    particle_pushes(ring, columns, sums, push_ref)
    for slot in range(4):
        back_ref[me * 4 + slot] = impulse_ref[me * 4 + slot, 0:3, :]

    def finish(turn, carry):
        step = order(turn)
        block_copy(step, outgoing, recv, data_out, data_in).wait()
        from_track, from_cross = peer_at(step, -1)
        source = from_track * 4 + from_cross
        for slot in range(4):
            back_ref[source * 4 + slot] = recv[source, slot * 3 : slot * 3 + 3, :]
        return carry

    lax.fori_loop(1, N_PEERS, finish, 0)


def last_kernel(state_ref, push_ref, later_ref, count_ref, back_ref, pos_ref, offset_ref, velocity_ref, impulse_ref):
    for row in range(2):
        for column in range(8):
            cell = row * 8 + column
            tile = advanced(state_ref[cell], push_ref[cell] + later_ref[cell], count_ref[row, column])
            for channel in range(3):
                offset_ref[channel, row, column : column + 1, :] = tile[channel : channel + 1]
                velocity_ref[channel, row, column : column + 1, :] = tile[channel + 3 : channel + 4]

    def one(block, carry):
        impulse_ref[block] = back_ref[pos_ref[block]]
        return carry

    lax.fori_loop(0, N_PEERS, one, 0, unroll=4)


def body(particle_offset, particle_velocity, cell_count, face_offset, face_velocity, face_route, face_cell):
    shape = jax.ShapeDtypeStruct
    tiles = shape((16, 8, 128), F32)
    limit = 48 * 1024 * 1024
    plain = pltpu.CompilerParams(vmem_limit_bytes=limit)

    def talking(name):
        return pltpu.CompilerParams(
            vmem_limit_bytes=limit, collective_id=name, has_side_effects=True
        )

    state, send, meta, pos = pl.pallas_call(
        pack_kernel,
        out_shape=(tiles, shape((64, 24, 128), F32), shape((64, 1, 128), jnp.int32), shape((64,), jnp.int32)),
        in_specs=[VM, VM, VM, VM, SM, SM],
        out_specs=(VM, VM, VM, SM),
        scratch_shapes=[pltpu.SMEM((64,), jnp.int32)],
        compiler_params=plain,
        name="pack",
    )(particle_offset, particle_velocity, face_offset, face_velocity, face_route, face_cell)

    cell_scratch = [
        pltpu.VMEM((16, 6, 128, 128), F32),
        pltpu.VMEM((16, 3, 128, 128), F32),
    ]
    sems = [pltpu.SemaphoreType.DMA((64,))] * 2
    halo_sems = [pltpu.SemaphoreType.DMA((8,))] * 2
    faces, cells, push = pl.pallas_call(
        first_kernel,
        out_shape=(shape((256, 8, 128), F32), shape((64, 1, 128), jnp.int32), tiles),
        in_specs=[VM, VM, VM, SM],
        out_specs=(VM, VM, VM),
        scratch_shapes=[
            pltpu.VMEM((64, 24, 128), F32),
            pltpu.VMEM((64, 1, 128), jnp.int32),
            pltpu.VMEM((4, 10, 8, 128), F32),
            *cell_scratch, *sems, *sems, *halo_sems,
        ],
        compiler_params=talking(0),
        name="exchange_faces",
    )(state, send, meta, cell_count)

    state, later, impulse = pl.pallas_call(
        face_kernel,
        out_shape=(tiles, tiles, shape((256, 8, 128), F32)),
        in_specs=[VM, SM, VM, VM, SM],
        out_specs=(VM, VM, VM),
        scratch_shapes=[
            *cell_scratch,
            pltpu.VMEM((16, 8, 128), F32),
            pltpu.VMEM((256, 8, 128), F32),
            pltpu.SMEM((264,), jnp.int32),
        ],
        compiler_params=plain,
        name="faces",
    )(faces, cells, state, push, cell_count)

    push, back = pl.pallas_call(
        second_kernel,
        out_shape=(tiles, shape((256, 3, 128), F32)),
        in_specs=[VM, VM, SM],
        out_specs=(VM, VM),
        scratch_shapes=[
            pltpu.VMEM((64, 12, 128), F32),
            pltpu.VMEM((64, 12, 128), F32),
            pltpu.VMEM((4, 10, 8, 128), F32),
            *cell_scratch, *sems, *halo_sems,
        ],
        compiler_params=talking(1),
        name="exchange_impulses",
    )(state, impulse, cell_count)

    return pl.pallas_call(
        last_kernel,
        out_shape=(
            shape(particle_offset.shape, F32),
            shape(particle_velocity.shape, F32),
            shape(face_offset.shape, F32),
        ),
        in_specs=[VM, VM, VM, SM, VM, SM],
        out_specs=(VM, VM, VM),
        compiler_params=plain,
        name="finish",
    )(state, push, later, cell_count, back, pos)


def solution(mesh):
    everyone = ("vehicle", "track", "cross")
    in_specs = (
        P(None, ("vehicle", "track"), "cross", None),
        P(None, ("vehicle", "track"), "cross", None),
        P(("vehicle", "track"), "cross"),
        P(everyone, None, None),
        P(everyone, None, None),
        P(everyone, None),
        P(everyone),
    )
    out_specs = (
        P(None, ("vehicle", "track"), "cross", None),
        P(None, ("vehicle", "track"), "cross", None),
        P(everyone, None, None),
    )
    return jax.shard_map(body, mesh=mesh, in_specs=in_specs, out_specs=out_specs, check_vma=False)
```

time: 276 us -> 162 us (0.59)
  Pallas kernels: 0 us -> 158 us
  other arithmetic: 114 us -> 0 us
  starting transfers between devices: 68.9 us -> 0 us
  waiting for transfers between devices: 51.8 us -> 0 us
  loops' own time: 22.3 us -> 0 us
  local copies, waits for them, and re-layouts: 11.5 us -> 3.8 us
  matrix products: 4.84 us -> 0 us
    pallas_call x0 -> x5, Pallas kernels: none -> 158 us  [the longest x1 87 us: body(): pl.pallas_call(second_kernel, out_shape=(tiles, shape((256, 3, 128), F32)...]
    reduce_sum x46 -> x0, other arithmetic: 91.3 us -> none  [the longest x16 32.2 us: contact(): jnp.sum((own_vel[:, :, :, None] - other_vel[:, :, None, :]) * normal, axi...]
    all_to_all x5 -> x0, starting transfers between devices: 49.5 us -> none  [the longest x2 21.1 us: body(): lax.all_to_all(outgoing.reshape(peers, capacity, 3, slot_count), ('track'...]
    ppermute x8 -> x0, waiting for transfers between devices: 43.5 us -> none  [the longest x4 23.7 us: with_halo(): lax.ppermute(lax.slice_in_dim(block, block.shape[dim] - width, None, axis...]
    another operation x4 -> x0, loops' own time: 22.3 us -> none  [the longest x2 21.6 us: particle_forces(): forces = lax.map(row_force, jnp.arange(stacked.shape[1], dtype=jnp.int32))]
    ppermute x8 -> x0, starting transfers between devices: 19.4 us -> none  [the longest x4 12.7 us: with_halo(): lax.ppermute(lax.slice_in_dim(block, block.shape[dim] - width, None, axis...]
    mul x45 -> x0, other arithmetic: 12.5 us -> none  [the longest x44 12.5 us: contact(): intersection * (stiffness - damping * closing) * other_live[:, None, :]]
    all_to_all x5 -> x0, waiting for transfers between devices: 8.33 us -> none  [the longest x1 8.32 us: body(): lax.all_to_all(requests.reshape(peers, capacity), ('track', 'cross'), spl...]
  transfers between devices with their start and end apart: 13 -> 0, of which waited for: 7 -> 0; matrix products, arithmetic and copies ran while one was open for 24% -> 0% of each run, Pallas kernels for 0% -> 0%
where the time goes in v1:
time: 162 us
  Pallas kernels  158 us (98%)
  local copies, waits for them, and re-layouts  3.8 us (2%)
    pallas_call x1, Pallas kernels, body(): pl.pallas_call(second_kernel, out_shape=(tiles, shape((256, 3, 128), F32)...  87 us
    pallas_call x1, Pallas kernels, body(): pl.pallas_call(first_kernel, out_shape=(shape((256, 8, 128), F32), shape(...  40.5 us
    pallas_call x1, Pallas kernels, body(): pl.pallas_call(face_kernel, out_shape=(tiles, tiles, shape((256, 8, 128),...  25.9 us

profile of v1, /device:TPU:1, one launch (start us, length us, event | category | flops | bytes accessed | tf_op | source)
XLA Modules:
  0.0 162.1 jit_solution(241578260158581065)
XLA Ops:
  0.6 0.7 copy.12.route_ref
  1.4 0.0 copy-start.4
  1.4 1.0 copy.10.fo_ref
  2.4 0.0 copy-done.4
  2.4 0.0 copy-start
  2.4 0.0 copy-start.1
  2.4 0.0 copy-start.3
  2.4 0.1 copy.11.fv_ref
  2.5 0.6 copy-done
  3.1 0.0 copy-done.1
  3.1 0.0 copy-done.3
  3.1 2.9 %pack.1 = (f32[16,8,128]{2,1,0:T(8,128)S(1)}, f32[64,24,128]{2,1,0:T(8,128)S(1)}, s32[64,1,128]{2,1,0:T(1,128)S(1)}, s32[64]{0:T(128)S(1)}) custom-call(f32[3,2,8,128]{3,2,1,0:T(8,128)S(1)} %copy-done, f32[3,2,8,128]{3,2,1,0:T(8,128)S(1)} %copy-done.1, f32[64,3,128]{2,1,0:T(4,128)S(1)} %copy.10.fo_ref, f32[64,3,128]{2,1,0:T(4,128)S(1)} %copy.11.fv_ref, ...), custom_call_target="tpu_custom_call" | custom-call | tf_op jit(solution)/shard_map/pack/pallas_call | solution.py:426
  6.0 0.0 copy-start.2
  6.0 0.7 copy-done.2
  6.7 40.5 %exchange_faces.1 = (f32[256,8,128]{2,1,0:T(8,128)S(1)}, s32[64,1,128]{2,1,0:T(1,128)S(1)}, f32[16,8,128]{2,1,0:T(8,128)S(1)}) custom-call(f32[16,8,128]{2,1,0:T(8,128)S(1)} %get-tuple-element.15.state_ref, f32[64,24,128]{2,1,0:T(8,128)S(1)} %get-tuple-element.16.send_ref, s32[64,1,128]{2,1,0:T(1,128)S(1)} %get-tuple-element.17.meta_ref, s32[2,8]{1,0:T(2,128)S(1)} %copy-done.2), custom_call_target="tpu_custom_call" | custom-call | tf_op jit(solution)/shard_map/exchange_faces/pallas_call | solution.py:442
  47.2 25.9 %faces.1 = (f32[16,8,128]{2,1,0:T(8,128)S(1)}, f32[16,8,128]{2,1,0:T(8,128)S(1)}, f32[256,8,128]{2,1,0:T(8,128)S(1)}) custom-call(f32[256,8,128]{2,1,0:T(8,128)S(1)} %get-tuple-element.18.faces_ref, s32[64,1,128]{2,1,0:T(1,128)S(1)} %get-tuple-element.19.cells_ref, f32[16,8,128]{2,1,0:T(8,128)S(1)} %get-tuple-element.15.state_ref, ...), custom_call_target="tpu_custom_call" | custom-call | tf_op jit(solution)/shard_map/faces/pallas_call | solution.py:457
  73.1 87.0 %exchange_impulses.1 = (f32[16,8,128]{2,1,0:T(8,128)S(1)}, f32[256,3,128]{2,1,0:T(4,128)S(1)}) custom-call(f32[16,8,128]{2,1,0:T(8,128)S(1)} %get-tuple-element.21.state_ref, f32[256,8,128]{2,1,0:T(8,128)S(1)} %get-tuple-element.22.impulse_ref, s32[2,8]{1,0:T(2,128)S(1)} %copy-done.2), custom_call_target="tpu_custom_call" | custom-call | tf_op jit(solution)/shard_map/exchange_impulses/pallas_call | solution.py:472
  160.2 1.3 finish.1
  161.5 0.6 copy.13
Async XLA Ops:
  1.4 1.0 copy-start.4
  2.4 0.7 copy-start
  2.4 0.7 copy-start.1
  2.4 0.7 copy-start.3
  6.0 0.7 copy-start.2

commit v2 on v1

--- a/solution.py
+++ b/solution.py
@@ -17,11 +17,13 @@
 away = 1.0e6
 
 F32 = jnp.float32
+BF16 = jnp.bfloat16
 MESH = pl.DeviceIdType.MESH
 VM = pl.BlockSpec(memory_space=pltpu.VMEM)
 SM = pl.BlockSpec(memory_space=pltpu.SMEM)
 SIDES = [(a, b) for a in (-1, 0, 1) for b in (-1, 0, 1) if (a, b) != (0, 0)]
 N_PEERS = 64
+WIDTH = 2
 
 
 def rows():
@@ -53,7 +55,7 @@
     x, y, z = (own[axis] - other[axis] for axis in range(3))
     square = x * x + (y * y + (z * z + soften * soften))
     inverse = lax.rsqrt(square)
-    depth = jnp.maximum(reach - square * inverse, 0.0) * inverse
+    depth = jnp.maximum(reach * inverse - 1.0, 0.0)
     closing = (own[3] - other[3]) * x + (own[4] - other[4]) * y + (own[5] - other[5]) * z
     weight = depth * (stiffness + closing * inverse)
     return weight * x, weight * y, weight * z
@@ -72,17 +74,18 @@
 
 def peer_at(step, sign):
     _, track, cross = place()
-    dz, dx, dc = step % 8, (step // 8) % 4, step // 32
-    x = (track // 4 + 4 + sign * dx) % 4
-    z = (cross * 2 + (track // 2) % 2 + 8 + sign * dz) % 8
-    core = (track % 2 + dc) % 2
-    return x * 4 + (z % 2) * 2 + core, z // 2
+    dz, rest = lax.rem(step, 8), lax.div(step, 8)
+    dx, dc = lax.rem(rest, 4), lax.div(rest, 4)
+    x = lax.rem(lax.div(track, 4) + 4 + sign * dx, 4)
+    z = lax.rem(cross * 2 + lax.rem(lax.div(track, 2), 2) + 8 + sign * dz, 8)
+    core = lax.rem(lax.rem(track, 2) + dc, 2)
+    return x * 4 + lax.rem(z, 2) * 2 + core, lax.div(z, 2)
 
 
 def neighbour(side):
     vehicle, track, cross = place()
-    row = (vehicle * 16 + track + 64 + side[0]) % 64
-    return row // 16, row % 16, (cross + 4 + side[1]) % 4
+    row = lax.rem(vehicle * 16 + track + 64 + side[0], 64)
+    return lax.div(row, 16), lax.rem(row, 16), lax.rem(cross + 4 + side[1], 4)
 
 
 def greet():
@@ -99,7 +102,10 @@
     for side in SIDES:
         pl.semaphore_signal(barrier, inc=1, device_id=neighbour(side), device_id_type=MESH)
     lax.fori_loop(1, N_PEERS, one, 0)
-    pl.semaphore_wait(barrier, N_PEERS - 1 + len(SIDES))
+
+
+def meet_all():
+    pl.semaphore_wait(pltpu.get_barrier_semaphore(), N_PEERS - 1 + len(SIDES))
 
 
 def halo_copy(index, ring, send_sem, recv_sem):
@@ -132,22 +138,31 @@
 
 
 def order(turn):
-    return (turn * 21) % 64
+    return lax.rem(turn * 21, 64)
+
+
+def parts3(tile):
+    high = tile.astype(BF16).astype(F32)
+    rest = tile - high
+    middle = rest.astype(BF16).astype(F32)
+    return high, middle, rest - middle
 
 
 def set_up_cells(state_ref, count_ref, columns_ref, ring_ref=None):
-    def one(cell, carry):
+    line = lax.broadcasted_iota(jnp.int32, (32, 768), 0)
+    lane = lax.broadcasted_iota(jnp.int32, (32, 768), 1)
+    chosen = (lax.rem(line, 8) == lax.div(lane, 128)) & (line < 24)
+    pick = jnp.where(chosen, 1.0, 0.0).astype(BF16)
+    for cell in range(16):
         alive = lanes() < count_ref[cell // 8, cell % 8]
         tile = scaled(state_ref[cell])
         own = jnp.where(alive, tile, resting(1.0))
+        stack = jnp.concatenate([*parts3(own), jnp.zeros((8, 128), F32)], axis=0)
+        wide = jnp.dot(stack.T.astype(BF16), pick, preferred_element_type=F32)
         for channel in range(6):
-            line = jnp.broadcast_to(own[channel : channel + 1], (128, 128))
-            columns_ref[cell, channel] = line.T
+            columns_ref[cell, channel] = wide[:, 128 * channel : 128 * channel + 128]
         if ring_ref is not None:
             ring_ref[cell // 8 + 1, cell % 8 + 1] = jnp.where(alive, tile, resting(-1.0))
-        return carry
-
-    lax.fori_loop(0, 16, one, 0)
 
 
 def clear_edges(ring_ref):
@@ -202,7 +217,7 @@
         out_ref[cell] = across_lanes(sums_ref, cell)
         return carry
 
-    lax.fori_loop(0, 16, gather, 0)
+    lax.fori_loop(0, 16, gather, 0, unroll=4)
 
 
 def pack_kernel(po_ref, pv_ref, fo_ref, fv_ref, route_ref, cell_ref, state_ref, send_ref, meta_ref, pos_ref, used):
@@ -244,8 +259,9 @@
 ):
     _, track, cross = place()
     me = track * 4 + cross
+    greet()
     set_up_cells(state_ref, count_ref, columns, ring)
-    greet()
+    meet_all()
     for index in range(8):
         halo_copy(index, ring, halo_out, halo_in).start()
 
@@ -262,6 +278,7 @@
     particle_pushes(ring, columns, sums, push_ref)
     for slot in range(4):
         faces_ref[me * 4 + slot, 0:6, :] = send_ref[me, slot * 6 : slot * 6 + 6, :]
+    faces_ref[256] = resting(-1.0)
     cells_ref[me] = meta_ref[me]
 
     def finish(turn, carry):
@@ -281,69 +298,89 @@
 def face_kernel(
     faces_ref, cells_ref, state_ref, push_ref, count_ref,
     next_ref, later_ref, impulse_ref,
-    columns, sums, total, reaction, listing,
+    columns, sums, now, filled, listing,
 ):
-    def gather(index, found):
-        listing[found] = index
-        return found + (cells_ref[index // 4, 0, index % 4] >= 0).astype(jnp.int32)
-
-    found = lax.fori_loop(0, 256, gather, 0, unroll=8)
-
-    def sweep(second_step):
+    room = 256 + WIDTH
+    for cell in range(17):
+        filled[cell] = 0
+
+    def enter(index, carry):
+        named = cells_ref[lax.div(index, 4), 0, lax.rem(index, 4)]
+        cell = jnp.where(named >= 0, named, 16)
+        count = filled[cell]
+        listing[cell * room + count] = index
+        filled[cell] = count + 1
+        return carry
+
+    lax.fori_loop(0, 256, enter, 0, unroll=4)
+    for cell in range(16):
+        for extra in range(WIDTH - 1):
+            listing[cell * room + filled[cell] + extra] = 256
+    now[...] = state_ref[...]
+
+    def substep(step, carry):
+        moved = time_step * step.astype(F32)
         sums[...] = jnp.zeros_like(sums)
-
-        def one(turn, carry):
-            slot = listing[turn]
-            cell = cells_ref[slot // 4, 0, slot % 4]
-            tile = faces_ref[slot]
-            row = rows()
-            tile = jnp.where(row < 6, tile, 0.0)
-            if second_step:
-                tile = tile + jnp.where(row < 3, time_step * roll(tile, 5), 0.0)
-            other = spread(scaled(tile))
-            spans = (count_ref[cell // 8, cell % 8] + 31) // 32
-
-            def meet(count):
-                back = [0.0, 0.0, 0.0]
+        set_up_cells(now, count_ref, columns)
+
+        def contacts(cell, count):
+            def one(turn, carry):
+                slots = [listing[cell * room + turn * WIDTH + index] for index in range(WIDTH)]
+                row = rows()
+                others = []
+                for slot in slots:
+                    tile = faces_ref[slot]
+                    tile = tile + jnp.where(row < 3, moved * roll(tile, 5), 0.0)
+                    others.append(spread(scaled(tile)))
+                back = [[0.0, 0.0, 0.0] for _ in slots]
                 for part in range(count):
                     span = slice(8 * part, 8 * part + 8)
                     own = [columns[cell, channel, span, :] for channel in range(6)]
-                    push = pushes(own, other, radius + face_radius)
+                    push = [pushes(own, other, radius + face_radius) for other in others]
                     for axis in range(3):
-                        sums[cell, axis, span, :] = sums[cell, axis, span, :] + push[axis]
-                        back[axis] = back[axis] + push[axis]
-                for axis in range(3):
-                    line = -time_step * jnp.sum(back[axis], axis=0, keepdims=True)
-                    if second_step:
-                        impulse_ref[slot, axis : axis + 1, :] = reaction[slot, axis : axis + 1, :] + line
-                    else:
-                        reaction[slot, axis : axis + 1, :] = line
-
-            for number in range(1, 5):
-                pl.when(spans == number)(functools.partial(meet, 4 * number))
+                        gained = push[0][axis]
+                        for other in push[1:]:
+                            gained = gained + other[axis]
+                        sums[cell, axis, span, :] = sums[cell, axis, span, :] + gained
+                        for side in range(WIDTH):
+                            back[side][axis] = back[side][axis] + push[side][axis]
+                for side in range(WIDTH):
+                    lines = [-time_step * jnp.sum(back[side][axis], axis=0, keepdims=True) for axis in range(3)]
+                    tile = jnp.concatenate(lines + [jnp.zeros((5, 128), F32)], axis=0)
+                    earlier = jnp.where(step == 0, 0.0, impulse_ref[slots[side]])
+                    impulse_ref[slots[side]] = earlier + tile
+                return carry
+
+            lax.fori_loop(0, lax.div(filled[cell] + WIDTH - 1, WIDTH), one, 0)
+
+        def block(cell, carry):
+            spans = lax.div(count_ref[lax.div(cell, 8), lax.rem(cell, 8)] + 15, 16)
+            for number in range(2, 9):
+                pl.when(spans == number)(functools.partial(contacts, cell, 2 * number))
             return carry
 
-        lax.fori_loop(0, found, one, 0)
+        lax.fori_loop(0, 16, block, 0)
 
         def collect(cell, carry):
-            total[cell] = across_lanes(sums, cell)
+            later_ref[cell] = across_lanes(sums, cell)
             return carry
 
-        lax.fori_loop(0, 16, collect, 0)
-
-    set_up_cells(state_ref, count_ref, columns)
-    sweep(False)
-
-    def advance(cell, carry):
-        next_ref[cell] = advanced(
-            state_ref[cell], push_ref[cell] + total[cell], count_ref[cell // 8, cell % 8]
-        )
-        return carry
-
-    lax.fori_loop(0, 16, advance, 0)
-    set_up_cells(next_ref, count_ref, columns)
-    sweep(True)
-    later_ref[...] = total[...]
+        lax.fori_loop(0, 16, collect, 0, unroll=4)
+
+        @pl.when(step == 0)
+        def _():
+            def advance(cell, carry):
+                count = count_ref[lax.div(cell, 8), lax.rem(cell, 8)]
+                tile = advanced(now[cell], push_ref[cell] + later_ref[cell], count)
+                now[cell] = tile
+                next_ref[cell] = tile
+                return carry
+
+            lax.fori_loop(0, 16, advance, 0, unroll=4)
+
+        return carry
+
+    lax.fori_loop(0, 2, substep, 0)
 
 
 def advanced(tile, push, count):
@@ -362,8 +399,9 @@
 ):
     _, track, cross = place()
     me = track * 4 + cross
+    greet()
     set_up_cells(state_ref, count_ref, columns, ring)
-    greet()
+    meet_all()
     for index in range(8):
         halo_copy(index, ring, halo_out, halo_in).start()
 
@@ -441,7 +479,7 @@
     halo_sems = [pltpu.SemaphoreType.DMA((8,))] * 2
     faces, cells, push = pl.pallas_call(
         first_kernel,
-        out_shape=(shape((256, 8, 128), F32), shape((64, 1, 128), jnp.int32), tiles),
+        out_shape=(shape((257, 8, 128), F32), shape((64, 1, 128), jnp.int32), tiles),
         in_specs=[VM, VM, VM, SM],
         out_specs=(VM, VM, VM),
         scratch_shapes=[
@@ -456,14 +494,14 @@
 
     state, later, impulse = pl.pallas_call(
         face_kernel,
-        out_shape=(tiles, tiles, shape((256, 8, 128), F32)),
+        out_shape=(tiles, tiles, shape((257, 8, 128), F32)),
         in_specs=[VM, SM, VM, VM, SM],
         out_specs=(VM, VM, VM),
         scratch_shapes=[
             *cell_scratch,
             pltpu.VMEM((16, 8, 128), F32),
-            pltpu.VMEM((256, 8, 128), F32),
-            pltpu.SMEM((264,), jnp.int32),
+            pltpu.SMEM((17,), jnp.int32),
+            pltpu.SMEM((17 * (256 + WIDTH),), jnp.int32),
         ],
         compiler_params=plain,
         name="faces",

time: 162 us -> 121 us (0.75)
  Pallas kernels: 158 us -> 114 us
  local copies, waits for them, and re-layouts: 3.8 us -> 6.12 us
    pallas_call x1, Pallas kernels: 87 us -> 56.1 us  [body(): pl.pallas_call(second_kernel, out_shape=(tiles, shape((256, 3, 128), F32)...]
    pallas_call x2, Pallas kernels: 66.4 us -> 53.2 us  [the longest x1 36.9 us: body(): pl.pallas_call(first_kernel, out_shape=(shape((257, 8, 128), F32), shape(...]
    unnamed x13 -> x11, local copies, waits for them, and re-layouts: 3.15 us -> 5.47 us
where the time goes in v2:
time: 121 us; the launch traced here: 120 us
  Pallas kernels  114 us (94%)
  local copies, waits for them, and re-layouts  6.12 us (5%)
    pallas_call x1, Pallas kernels, body(): pl.pallas_call(second_kernel, out_shape=(tiles, shape((256, 3, 128), F32)...  56.1 us
    pallas_call x1, Pallas kernels, body(): pl.pallas_call(first_kernel, out_shape=(shape((257, 8, 128), F32), shape(...  36.9 us
    pallas_call x1, Pallas kernels, body(): pl.pallas_call(face_kernel, out_shape=(tiles, tiles, shape((257, 8, 128),...  16.3 us
    unnamed x11, local copies, waits for them, and re-layouts  5.47 us
    pallas_call x1, Pallas kernels, body(): pl.pallas_call(pack_kernel, out_shape=(tiles, shape((64, 24, 128), F32),...  2.85 us

profile of v2, /device:TPU:1, one launch (start us, length us, event | category | flops | bytes accessed | tf_op | source)
XLA Modules:
  0.0 120.3 jit_solution(16221499249559271310)
XLA Ops:
  0.6 0.7 copy.12.route_ref
  1.4 1.0 copy.10.fo_ref
  2.3 1.0 copy.11.fv_ref
  3.3 0.0 copy-start
  3.3 0.7 copy-done
  4.0 0.0 copy-start.1
  4.0 0.7 copy-done.1
  4.8 0.0 copy-start.3
  4.8 0.7 copy-done.3
  5.4 2.9 %pack.1 = (f32[16,8,128]{2,1,0:T(8,128)S(1)}, f32[64,24,128]{2,1,0:T(8,128)S(1)}, s32[64,1,128]{2,1,0:T(1,128)S(1)}, s32[64]{0:T(128)S(1)}) custom-call(f32[3,2,8,128]{3,2,1,0:T(8,128)S(1)} %copy-done, f32[3,2,8,128]{3,2,1,0:T(8,128)S(1)} %copy-done.1, f32[64,3,128]{2,1,0:T(4,128)S(1)} %copy.10.fo_ref, f32[64,3,128]{2,1,0:T(4,128)S(1)} %copy.11.fv_ref, ...), custom_call_target="tpu_custom_call" | custom-call | tf_op jit(solution)/shard_map/pack/pallas_call | solution.py:464
  8.3 0.0 copy-start.2
  8.3 0.7 copy-done.2
  9.0 36.9 %exchange_faces.1 = (f32[257,8,128]{2,1,0:T(8,128)S(1)}, s32[64,1,128]{2,1,0:T(1,128)S(1)}, f32[16,8,128]{2,1,0:T(8,128)S(1)}) custom-call(f32[16,8,128]{2,1,0:T(8,128)S(1)} %get-tuple-element.15.state_ref, f32[64,24,128]{2,1,0:T(8,128)S(1)} %get-tuple-element.16.send_ref, s32[64,1,128]{2,1,0:T(1,128)S(1)} %get-tuple-element.17.meta_ref, s32[2,8]{1,0:T(2,128)S(1)} %copy-done.2), custom_call_target="tpu_custom_call" | custom-call | tf_op jit(solution)/shard_map/exchange_faces/pallas_call | solution.py:480
  45.9 16.3 %faces.1 = (f32[16,8,128]{2,1,0:T(8,128)S(1)}, f32[16,8,128]{2,1,0:T(8,128)S(1)}, f32[257,8,128]{2,1,0:T(8,128)S(1)}) custom-call(f32[257,8,128]{2,1,0:T(8,128)S(1)} %get-tuple-element.18.faces_ref, s32[64,1,128]{2,1,0:T(1,128)S(1)} %get-tuple-element.19.cells_ref, f32[16,8,128]{2,1,0:T(8,128)S(1)} %get-tuple-element.15.state_ref, ...), custom_call_target="tpu_custom_call" | custom-call | tf_op jit(solution)/shard_map/faces/pallas_call | solution.py:495
  62.2 56.1 %exchange_impulses.1 = (f32[16,8,128]{2,1,0:T(8,128)S(1)}, f32[256,3,128]{2,1,0:T(4,128)S(1)}) custom-call(f32[16,8,128]{2,1,0:T(8,128)S(1)} %get-tuple-element.21.state_ref, f32[257,8,128]{2,1,0:T(8,128)S(1)} %get-tuple-element.22.impulse_ref, s32[2,8]{1,0:T(2,128)S(1)} %copy-done.2), custom_call_target="tpu_custom_call" | custom-call | tf_op jit(solution)/shard_map/exchange_impulses/pallas_call | solution.py:510
  118.4 1.3 %finish.1 = (f32[3,2,8,128]{3,2,1,0:T(8,128)}, f32[3,2,8,128]{3,2,1,0:T(8,128)}, f32[64,3,128]{2,1,0:T(4,128)S(1)}) custom-call(f32[16,8,128]{2,1,0:T(8,128)S(1)} %get-tuple-element.21.state_ref, f32[16,8,128]{2,1,0:T(8,128)S(1)} %get-tuple-element.23.push_ref, f32[16,8,128]{2,1,0:T(8,128)S(1)} %get-tuple-element.24.later_ref, s32[2,8]{1,0:T(2,128)S(1)} %copy-done.2, ...), custom_call_target="tpu_custom_call" | custom-call | tf_op jit(solution)/shard_map/finish/pallas_call | solution.py:525
  119.7 0.6 copy.13
Async XLA Ops:
  3.3 0.7 copy-start
  4.0 0.7 copy-start.1
  4.8 0.7 copy-start.3
  8.3 0.7 copy-start.2

commit v3 on v2

--- a/solution.py
+++ b/solution.py
@@ -23,6 +23,8 @@
 SM = pl.BlockSpec(memory_space=pltpu.SMEM)
 SIDES = [(a, b) for a in (-1, 0, 1) for b in (-1, 0, 1) if (a, b) != (0, 0)]
 N_PEERS = 64
+COUNTS = 128
+PART = 2
 WIDTH = 2
 
 
@@ -42,9 +44,9 @@
     return jnp.where(rows() == 2, sign * away, 0.0)
 
 
-def scaled(tile):
+def scaled(tile, reach):
     row = rows()
-    return jnp.where(row < 3, tile, jnp.where(row < 6, -damping * tile, 0.0))
+    return jnp.where(row < 3, tile, jnp.where(row < 6, (-damping * reach) * tile, 0.0))
 
 
 def spread(tile):
@@ -55,9 +57,9 @@
     x, y, z = (own[axis] - other[axis] for axis in range(3))
     square = x * x + (y * y + (z * z + soften * soften))
     inverse = lax.rsqrt(square)
-    depth = jnp.maximum(reach * inverse - 1.0, 0.0)
+    depth = jnp.maximum(inverse - 1.0 / reach, 0.0)
     closing = (own[3] - other[3]) * x + (own[4] - other[4]) * y + (own[5] - other[5]) * z
-    weight = depth * (stiffness + closing * inverse)
+    weight = depth * (stiffness * reach + closing * inverse)
     return weight * x, weight * y, weight * z
 
 
@@ -148,14 +150,14 @@
     return high, middle, rest - middle
 
 
-def set_up_cells(state_ref, count_ref, columns_ref, ring_ref=None):
+def set_up_cells(state_ref, count_ref, reach, columns_ref, ring_ref=None):
     line = lax.broadcasted_iota(jnp.int32, (32, 768), 0)
     lane = lax.broadcasted_iota(jnp.int32, (32, 768), 1)
     chosen = (lax.rem(line, 8) == lax.div(lane, 128)) & (line < 24)
     pick = jnp.where(chosen, 1.0, 0.0).astype(BF16)
     for cell in range(16):
-        alive = lanes() < count_ref[cell // 8, cell % 8]
-        tile = scaled(state_ref[cell])
+        alive = lanes() < count_ref[COUNTS + cell]
+        tile = scaled(state_ref[cell], reach)
         own = jnp.where(alive, tile, resting(1.0))
         stack = jnp.concatenate([*parts3(own), jnp.zeros((8, 128), F32)], axis=0)
         wide = jnp.dot(stack.T.astype(BF16), pick, preferred_element_type=F32)
@@ -191,27 +193,64 @@
             ring_ref[row, 9] = dead
 
 
-def particle_pushes(ring_ref, columns_ref, sums_ref, out_ref):
-    width = 2
+def meet_blocks(cell, part, blocks, columns_ref, ring_ref, sums_ref, base_ref):
+    for piece in range(PART):
+        start = pl.multiple_of(part * (8 * PART) + 8 * piece, 8)
+        own = [columns_ref[cell, channel, pl.ds(start, 8), :] for channel in range(6)]
+        total = [0.0, 0.0, 0.0]
+        for row, column, down, right in blocks:
+            other = spread(ring_ref[row, column])
+            shifted = [own[0] - down, own[1] - right] + own[2:]
+            push = pushes(shifted, other, 2.0 * radius)
+            total = [total[axis] + push[axis] for axis in range(3)]
+        for axis in range(3):
+            if base_ref is not None:
+                total[axis] = total[axis] + base_ref[cell, axis, pl.ds(start, 8), :]
+            sums_ref[cell, axis, pl.ds(start, 8), :] = total[axis]
+
+
+def inner_pushes(ring_ref, columns_ref, sums_ref, base_ref=None):
+    parts = 16 // PART
 
     def one(turn, carry):
-        cell = turn // (16 // width)
-        row_index, column = cell // 8, cell % 8
-        for part in range(width):
-            start = pl.multiple_of((turn % (16 // width)) * (8 * width) + 8 * part, 8)
-            own = [columns_ref[cell, channel, pl.ds(start, 8), :] for channel in range(6)]
-            total = [0.0, 0.0, 0.0]
-            for down in (-1, 0, 1):
-                for right in (-1, 0, 1):
-                    other = spread(ring_ref[row_index + 1 + down, column + 1 + right])
-                    shifted = [own[0] - float(down), own[1] - float(right)] + own[2:]
-                    push = pushes(shifted, other, 2.0 * radius)
-                    total = [total[axis] + push[axis] for axis in range(3)]
-            for axis in range(3):
-                sums_ref[cell, axis, pl.ds(start, 8), :] = total[axis]
-        return carry
-
-    lax.fori_loop(0, 256 // width, one, 0)
+        which, part = lax.div(turn, parts), lax.rem(turn, parts)
+        row, column = lax.div(which, 6), lax.rem(which, 6) + 1
+        blocks = [
+            (other + 1, column + 1 + right, (other - row).astype(F32), float(right))
+            for other in range(2)
+            for right in (-1, 0, 1)
+        ]
+        meet_blocks(row * 8 + column, part, blocks, columns_ref, ring_ref, sums_ref, base_ref)
+        return carry
+
+    lax.fori_loop(0, 12 * parts, one, 0)
+
+
+def outer_pushes(ring_ref, columns_ref, sums_ref, out_ref, base_ref=None):
+    parts = 16 // PART
+
+    def one(turn, carry):
+        which, part = lax.div(turn, parts), lax.rem(turn, parts)
+        row, column = lax.div(which, 6), lax.rem(which, 6) + 1
+        down = (2 * row - 1).astype(F32)
+        blocks = [(3 * row, column + 1 + right, down, float(right)) for right in (-1, 0, 1)]
+        meet_blocks(row * 8 + column, part, blocks, columns_ref, ring_ref, sums_ref, sums_ref)
+        return carry
+
+    lax.fori_loop(0, 12 * parts, one, 0)
+
+    def side(turn, carry):
+        which, part = lax.div(turn, parts), lax.rem(turn, parts)
+        row, column = lax.div(which, 2), lax.rem(which, 2) * 7
+        blocks = [
+            (row + 1 + down, column + 1 + right, float(down), float(right))
+            for down in (-1, 0, 1)
+            for right in (-1, 0, 1)
+        ]
+        meet_blocks(row * 8 + column, part, blocks, columns_ref, ring_ref, sums_ref, base_ref)
+        return carry
+
+    lax.fori_loop(0, 4 * parts, side, 0)
 
     def gather(cell, carry):
         out_ref[cell] = across_lanes(sums_ref, cell)
@@ -220,76 +259,74 @@
     lax.fori_loop(0, 16, gather, 0, unroll=4)
 
 
-def pack_kernel(po_ref, pv_ref, fo_ref, fv_ref, route_ref, cell_ref, state_ref, send_ref, meta_ref, pos_ref, used):
+def pack_kernel(parts_ref, blocks_ref, ints_ref, state_ref, send_ref, pos_ref, used):
+    send_ref[:, 24:25, :] = jnp.full((N_PEERS, 1, 128), -1.0, F32)
+
+    def clear(index, carry):
+        used[index] = 0
+        return carry
+
+    lax.fori_loop(0, N_PEERS, clear, 0, unroll=8)
     for row in range(2):
         for column in range(8):
             cell = row * 8 + column
-            for channel in range(3):
-                state_ref[cell, channel : channel + 1, :] = po_ref[channel, row, column : column + 1, :]
-                state_ref[cell, channel + 3 : channel + 4, :] = pv_ref[channel, row, column : column + 1, :]
+            for channel in range(6):
+                state_ref[cell, channel : channel + 1, :] = parts_ref[channel, row, column : column + 1, :]
             state_ref[cell, 6:8, :] = jnp.zeros((2, 128), F32)
-    meta_ref[...] = jnp.full(meta_ref.shape, -1, jnp.int32)
-
-    def clear(index, carry):
-        used[index] = 0
-        return carry
-
-    lax.fori_loop(0, N_PEERS, clear, 0)
     lane = lax.broadcasted_iota(jnp.int32, (1, 128), 1)
 
     def one(block, carry):
-        target = route_ref[block, 0]
+        target = ints_ref[block]
         slot = used[target]
         used[target] = slot + 1
         pos_ref[block] = target * 4 + slot
-        meta_ref[target] = jnp.where(lane == slot, cell_ref[block], meta_ref[target])
-        for channel in range(3):
-            send_ref[target, pl.ds(slot * 6 + channel, 1), :] = fo_ref[block, channel : channel + 1, :]
-            send_ref[target, pl.ds(slot * 6 + 3 + channel, 1), :] = fv_ref[block, channel : channel + 1, :]
-        return carry
-
-    lax.fori_loop(0, N_PEERS, one, 0)
+        touched = ints_ref[N_PEERS + block].astype(F32)
+        send_ref[target, 24:25, :] = jnp.where(lane == slot, touched, send_ref[target, 24:25, :])
+        for channel in range(6):
+            send_ref[target, pl.ds(slot * 6 + channel, 1), :] = blocks_ref[channel, pl.ds(block, 1), :]
+        return carry
+
+    lax.fori_loop(0, N_PEERS, one, 0, unroll=4)
 
 
 def first_kernel(
-    state_ref, send_ref, meta_ref, count_ref,
+    state_ref, send_ref, count_ref,
     faces_ref, cells_ref, push_ref,
-    recv, recv_meta, ring, columns, sums,
-    data_out, data_in, meta_out, meta_in, halo_out, halo_in,
+    recv, ring, columns, sums,
+    data_out, data_in, halo_out, halo_in,
 ):
     _, track, cross = place()
     me = track * 4 + cross
     greet()
-    set_up_cells(state_ref, count_ref, columns, ring)
+    set_up_cells(state_ref, count_ref, 2.0 * radius, columns, ring)
     meet_all()
     for index in range(8):
         halo_copy(index, ring, halo_out, halo_in).start()
 
     def start(turn, carry):
         step = order(turn)
-        block_copy(step, meta_ref, recv_meta, meta_out, meta_in).start()
         block_copy(step, send_ref, recv, data_out, data_in).start()
         return carry
 
     lax.fori_loop(1, N_PEERS, start, 0)
+    inner_pushes(ring, columns, sums)
     for index in range(8):
         halo_copy(index, ring, halo_out, halo_in).wait()
     clear_edges(ring)
-    particle_pushes(ring, columns, sums, push_ref)
+    outer_pushes(ring, columns, sums, push_ref)
     for slot in range(4):
         faces_ref[me * 4 + slot, 0:6, :] = send_ref[me, slot * 6 : slot * 6 + 6, :]
     faces_ref[256] = resting(-1.0)
-    cells_ref[me] = meta_ref[me]
+    cells_ref[me] = send_ref[me, 24:25, :]
 
     def finish(turn, carry):
         step = order(turn)
-        block_copy(step, meta_ref, recv_meta, meta_out, meta_in).wait()
         block_copy(step, send_ref, recv, data_out, data_in).wait()
         from_track, from_cross = peer_at(step, -1)
         source = from_track * 4 + from_cross
         for slot in range(4):
             faces_ref[source * 4 + slot, 0:6, :] = recv[source, slot * 6 : slot * 6 + 6, :]
-        cells_ref[source] = recv_meta[source]
+        cells_ref[source] = recv[source, 24:25, :]
         return carry
 
     lax.fori_loop(1, N_PEERS, finish, 0)
@@ -297,15 +334,15 @@
 
 def face_kernel(
     faces_ref, cells_ref, state_ref, push_ref, count_ref,
-    next_ref, later_ref, impulse_ref,
-    columns, sums, now, filled, listing,
+    next_ref, sums, impulse_ref,
+    columns, now, filled, listing,
 ):
     room = 256 + WIDTH
     for cell in range(17):
         filled[cell] = 0
 
     def enter(index, carry):
-        named = cells_ref[lax.div(index, 4), 0, lax.rem(index, 4)]
+        named = cells_ref[lax.div(index, 4), 0, lax.rem(index, 4)].astype(jnp.int32)
         cell = jnp.where(named >= 0, named, 16)
         count = filled[cell]
         listing[cell * room + count] = index
@@ -321,7 +358,7 @@
     def substep(step, carry):
         moved = time_step * step.astype(F32)
         sums[...] = jnp.zeros_like(sums)
-        set_up_cells(now, count_ref, columns)
+        set_up_cells(now, count_ref, radius + face_radius, columns)
 
         def contacts(cell, count):
             def one(turn, carry):
@@ -331,7 +368,7 @@
                 for slot in slots:
                     tile = faces_ref[slot]
                     tile = tile + jnp.where(row < 3, moved * roll(tile, 5), 0.0)
-                    others.append(spread(scaled(tile)))
+                    others.append(spread(scaled(tile, radius + face_radius)))
                 back = [[0.0, 0.0, 0.0] for _ in slots]
                 for part in range(count):
                     span = slice(8 * part, 8 * part + 8)
@@ -354,24 +391,18 @@
             lax.fori_loop(0, lax.div(filled[cell] + WIDTH - 1, WIDTH), one, 0)
 
         def block(cell, carry):
-            spans = lax.div(count_ref[lax.div(cell, 8), lax.rem(cell, 8)] + 15, 16)
-            for number in range(2, 9):
-                pl.when(spans == number)(functools.partial(contacts, cell, 2 * number))
+            spans = lax.div(count_ref[COUNTS + cell] + 7, 8)
+            for number in range(4, 17):
+                pl.when(spans == number)(functools.partial(contacts, cell, number))
             return carry
 
         lax.fori_loop(0, 16, block, 0)
-
-        def collect(cell, carry):
-            later_ref[cell] = across_lanes(sums, cell)
-            return carry
-
-        lax.fori_loop(0, 16, collect, 0, unroll=4)
 
         @pl.when(step == 0)
         def _():
             def advance(cell, carry):
-                count = count_ref[lax.div(cell, 8), lax.rem(cell, 8)]
-                tile = advanced(now[cell], push_ref[cell] + later_ref[cell], count)
+                total = push_ref[cell] + across_lanes(sums, cell)
+                tile = advanced(now[cell], total, count_ref[COUNTS + cell])
                 now[cell] = tile
                 next_ref[cell] = tile
                 return carry
@@ -392,7 +423,7 @@
 
 
 def second_kernel(
-    state_ref, impulse_ref, count_ref,
+    state_ref, impulse_ref, base_ref, count_ref,
     push_ref, back_ref,
     outgoing, recv, ring, columns, sums,
     data_out, data_in, halo_out, halo_in,
@@ -400,7 +431,7 @@
     _, track, cross = place()
     me = track * 4 + cross
     greet()
-    set_up_cells(state_ref, count_ref, columns, ring)
+    set_up_cells(state_ref, count_ref, 2.0 * radius, columns, ring)
     meet_all()
     for index in range(8):
         halo_copy(index, ring, halo_out, halo_in).start()
@@ -415,10 +446,11 @@
         return carry
 
     lax.fori_loop(1, N_PEERS, start, 0)
+    inner_pushes(ring, columns, sums, base_ref)
     for index in range(8):
         halo_copy(index, ring, halo_out, halo_in).wait()
     clear_edges(ring)
-    particle_pushes(ring, columns, sums, push_ref)
+    outer_pushes(ring, columns, sums, push_ref, base_ref)
     for slot in range(4):
         back_ref[me * 4 + slot] = impulse_ref[me * 4 + slot, 0:3, :]
 
@@ -434,17 +466,19 @@
     lax.fori_loop(1, N_PEERS, finish, 0)
 
 
-def last_kernel(state_ref, push_ref, later_ref, count_ref, back_ref, pos_ref, offset_ref, velocity_ref, impulse_ref):
+def last_kernel(state_ref, push_ref, count_ref, back_ref, pos_ref, offset_ref, velocity_ref, impulse_ref):
     for row in range(2):
         for column in range(8):
             cell = row * 8 + column
-            tile = advanced(state_ref[cell], push_ref[cell] + later_ref[cell], count_ref[row, column])
+            tile = advanced(state_ref[cell], push_ref[cell], count_ref[COUNTS + cell])
             for channel in range(3):
                 offset_ref[channel, row, column : column + 1, :] = tile[channel : channel + 1]
                 velocity_ref[channel, row, column : column + 1, :] = tile[channel + 3 : channel + 4]
 
     def one(block, carry):
-        impulse_ref[block] = back_ref[pos_ref[block]]
+        slot = pos_ref[block]
+        for axis in range(3):
+            impulse_ref[axis, pl.ds(block, 1), :] = back_ref[slot, axis : axis + 1, :]
         return carry
 
     lax.fori_loop(0, N_PEERS, one, 0, unroll=4)
@@ -461,15 +495,20 @@
             vmem_limit_bytes=limit, collective_id=name, has_side_effects=True
         )
 
-    state, send, meta, pos = pl.pallas_call(
+    parts = jnp.concatenate([particle_offset, particle_velocity], axis=0)
+    blocks = jnp.concatenate(
+        [jnp.transpose(face_offset, (1, 0, 2)), jnp.transpose(face_velocity, (1, 0, 2))], axis=0
+    )
+    ints = jnp.concatenate([face_route.reshape(-1), face_cell, cell_count.reshape(-1)])
+    state, send, pos = pl.pallas_call(
         pack_kernel,
-        out_shape=(tiles, shape((64, 24, 128), F32), shape((64, 1, 128), jnp.int32), shape((64,), jnp.int32)),
-        in_specs=[VM, VM, VM, VM, SM, SM],
-        out_specs=(VM, VM, VM, SM),
+        out_shape=(tiles, shape((64, 25, 128), F32), shape((64,), jnp.int32)),
+        in_specs=[VM, VM, SM],
+        out_specs=(VM, VM, SM),
         scratch_shapes=[pltpu.SMEM((64,), jnp.int32)],
         compiler_params=plain,
         name="pack",
-    )(particle_offset, particle_velocity, face_offset, face_velocity, face_route, face_cell)
+    )(parts, blocks, ints)
 
     cell_scratch = [
         pltpu.VMEM((16, 6, 128, 128), F32),
@@ -479,38 +518,37 @@
     halo_sems = [pltpu.SemaphoreType.DMA((8,))] * 2
     faces, cells, push = pl.pallas_call(
         first_kernel,
-        out_shape=(shape((257, 8, 128), F32), shape((64, 1, 128), jnp.int32), tiles),
-        in_specs=[VM, VM, VM, SM],
+        out_shape=(shape((257, 8, 128), F32), shape((64, 1, 128), F32), tiles),
+        in_specs=[VM, VM, SM],
         out_specs=(VM, VM, VM),
         scratch_shapes=[
-            pltpu.VMEM((64, 24, 128), F32),
-            pltpu.VMEM((64, 1, 128), jnp.int32),
+            pltpu.VMEM((64, 25, 128), F32),
             pltpu.VMEM((4, 10, 8, 128), F32),
-            *cell_scratch, *sems, *sems, *halo_sems,
+            *cell_scratch, *sems, *halo_sems,
         ],
         compiler_params=talking(0),
         name="exchange_faces",
-    )(state, send, meta, cell_count)
-
-    state, later, impulse = pl.pallas_call(
+    )(state, send, ints)
+
+    state, sums, impulse = pl.pallas_call(
         face_kernel,
-        out_shape=(tiles, tiles, shape((257, 8, 128), F32)),
+        out_shape=(tiles, shape((16, 3, 128, 128), F32), shape((257, 8, 128), F32)),
         in_specs=[VM, SM, VM, VM, SM],
         out_specs=(VM, VM, VM),
         scratch_shapes=[
-            *cell_scratch,
+            cell_scratch[0],
             pltpu.VMEM((16, 8, 128), F32),
             pltpu.SMEM((17,), jnp.int32),
             pltpu.SMEM((17 * (256 + WIDTH),), jnp.int32),
         ],
         compiler_params=plain,
         name="faces",
-    )(faces, cells, state, push, cell_count)
+    )(faces, cells, state, push, ints)
 
     push, back = pl.pallas_call(
         second_kernel,
         out_shape=(tiles, shape((256, 3, 128), F32)),
-        in_specs=[VM, VM, SM],
+        in_specs=[VM, VM, VM, SM],
         out_specs=(VM, VM),
         scratch_shapes=[
             pltpu.VMEM((64, 12, 128), F32),
@@ -520,20 +558,21 @@
         ],
         compiler_params=talking(1),
         name="exchange_impulses",
-    )(state, impulse, cell_count)
-
-    return pl.pallas_call(
+    )(state, impulse, sums, ints)
+
+    offset, velocity, impulse = pl.pallas_call(
         last_kernel,
         out_shape=(
             shape(particle_offset.shape, F32),
             shape(particle_velocity.shape, F32),
-            shape(face_offset.shape, F32),
+            shape((3, 64, 128), F32),
         ),
-        in_specs=[VM, VM, VM, SM, VM, SM],
+        in_specs=[VM, VM, SM, VM, SM],
         out_specs=(VM, VM, VM),
         compiler_params=plain,
         name="finish",
-    )(state, push, later, cell_count, back, pos)
+    )(state, push, ints, back, pos)
+    return offset, velocity, jnp.transpose(impulse, (1, 0, 2))
 
 
 def solution(mesh):

time: 121 us -> 113 us (0.934)
  local copies, waits for them, and re-layouts: 6.12 us -> 0.76 us
  Pallas kernels: 114 us -> 109 us
  other arithmetic: 0 us -> 2.46 us
    unnamed x11 -> x0, local copies, waits for them, and re-layouts: 5.47 us -> none
    concatenate x0 -> x3, other arithmetic: none -> 2.46 us  [the longest x1 0.95 us: body(): jnp.concatenate([jnp.transpose(face_offset, (1, 0, 2)), jnp.transpose(fac...]
    pallas_call x1, Pallas kernels: 56.1 us -> 54.3 us  [body(): pl.pallas_call(second_kernel, out_shape=(tiles, shape((256, 3, 128), F32)...]
    pallas_call x2, Pallas kernels: 19.2 us -> 17.6 us  [the longest x1 15.9 us: body(): pl.pallas_call(face_kernel, out_shape=(tiles, shape((16, 3, 128, 128), F3...]
where the time goes in v3:
time: 113 us
  Pallas kernels  109 us (96%)
  other arithmetic  2.46 us (2%)
    pallas_call x1, Pallas kernels, body(): pl.pallas_call(second_kernel, out_shape=(tiles, shape((256, 3, 128), F32)...  54.3 us
    pallas_call x1, Pallas kernels, body(): pl.pallas_call(first_kernel, out_shape=(shape((257, 8, 128), F32), shape(...  35.8 us
    pallas_call x1, Pallas kernels, body(): pl.pallas_call(face_kernel, out_shape=(tiles, shape((16, 3, 128, 128), F3...  15.9 us

profile of v3, /device:TPU:1, one launch (start us, length us, event | category | flops | bytes accessed | tf_op | source)
XLA Modules:
  0.0 113.0 jit_solution(9894402703752410913)
XLA Ops:
  0.6 0.8 reshape.13
  1.4 0.7 pad_add_fusion.ints_ref.count_ref
  2.1 0.8 pad_maximum_fusion.1.parts_ref
  2.9 1.0 pad_maximum_fusion.blocks_ref
  3.9 1.7 %pack.1 = (f32[16,8,128]{2,1,0:T(8,128)S(1)}, f32[64,25,128]{2,1,0:T(8,128)S(1)}, s32[64]{0:T(128)S(1)}) custom-call(f32[6,2,8,128]{3,2,1,0:T(8,128)S(1)} %pad_maximum_fusion.1.parts_ref, f32[6,64,128]{2,1,0:T(8,128)S(1)} %pad_maximum_fusion.blocks_ref, s32[144]{0:T(256)S(1)} %pad_add_fusion.ints_ref.count_ref), custom_call_target="tpu_custom_call" | custom-call | tf_op jit(solution)/shard_map/pack/pallas_call | solution.py:503
  5.6 35.8 %exchange_faces.1 = (f32[257,8,128]{2,1,0:T(8,128)S(1)}, f32[64,1,128]{2,1,0:T(1,128)S(1)}, f32[16,8,128]{2,1,0:T(8,128)S(1)}) custom-call(f32[16,8,128]{2,1,0:T(8,128)S(1)} %get-tuple-element.17.state_ref, f32[64,25,128]{2,1,0:T(8,128)S(1)} %get-tuple-element.18.send_ref, s32[144]{0:T(256)S(1)} %pad_add_fusion.ints_ref.count_ref), custom_call_target="tpu_custom_call" | custom-call | tf_op jit(solution)/shard_map/exchange_faces/pallas_call | solution.py:519
  41.4 15.9 %faces.1 = (f32[16,8,128]{2,1,0:T(8,128)S(1)}, f32[16,3,128,128]{3,2,1,0:T(8,128)S(1)}, f32[257,8,128]{2,1,0:T(8,128)S(1)}) custom-call(f32[257,8,128]{2,1,0:T(8,128)S(1)} %get-tuple-element.19.faces_ref, f32[64,1,128]{2,1,0:T(1,128)S(1)} %get-tuple-element.20.cells_ref, f32[16,8,128]{2,1,0:T(8,128)S(1)} %get-tuple-element.17.state_ref, ...), custom_call_target="tpu_custom_call" | custom-call | tf_op jit(solution)/shard_map/faces/pallas_call | solution.py:533
  57.3 54.3 %exchange_impulses.1 = (f32[16,8,128]{2,1,0:T(8,128)S(1)}, f32[256,3,128]{2,1,0:T(4,128)S(1)}) custom-call(f32[16,8,128]{2,1,0:T(8,128)S(1)} %get-tuple-element.22.state_ref, f32[257,8,128]{2,1,0:T(8,128)S(1)} %get-tuple-element.23.impulse_ref, f32[16,3,128,128]{3,2,1,0:T(8,128)S(1)} %get-tuple-element.24.base_ref, s32[144]{0:T(256)S(1)} %pad_add_fusion.ints_ref.count_ref), custom_call_target="tpu_custom_call" | custom-call | tf_op jit(solution)/shard_map/exchange_impulses/pallas_call | solution.py:548
  111.6 1.4 %finish.1 = (f32[3,2,8,128]{3,2,1,0:T(8,128)}, f32[3,2,8,128]{3,2,1,0:T(8,128)}, f32[3,64,128]{2,1,0:T(8,128)}) custom-call(f32[16,8,128]{2,1,0:T(8,128)S(1)} %get-tuple-element.22.state_ref, f32[16,8,128]{2,1,0:T(8,128)S(1)} %get-tuple-element.25.push_ref, s32[144]{0:T(256)S(1)} %pad_add_fusion.ints_ref.count_ref, ...), custom_call_target="tpu_custom_call" | custom-call | tf_op jit(solution)/shard_map/finish/pallas_call | solution.py:563

commit v4 on v3

--- a/solution.py
+++ b/solution.py
@@ -204,56 +204,80 @@
             push = pushes(shifted, other, 2.0 * radius)
             total = [total[axis] + push[axis] for axis in range(3)]
         for axis in range(3):
-            if base_ref is not None:
-                total[axis] = total[axis] + base_ref[cell, axis, pl.ds(start, 8), :]
+            total[axis] = total[axis] + base_ref[cell, axis, pl.ds(start, 8), :]
             sums_ref[cell, axis, pl.ds(start, 8), :] = total[axis]
 
 
-def inner_pushes(ring_ref, columns_ref, sums_ref, base_ref=None):
+def own_pushes(row, column, partners, columns_ref, ring_ref, sums_ref, out_ref, base_ref):
+    cell = row * 8 + column
+
+    def one(part, carry):
+        back = list(carry)
+        for piece in range(PART):
+            start = pl.multiple_of(part * (8 * PART) + 8 * piece, 8)
+            own = [columns_ref[cell, channel, pl.ds(start, 8), :] for channel in range(6)]
+            total = list(pushes(own, spread(ring_ref[row + 1, column + 1]), 2.0 * radius))
+            for index, (down, right) in enumerate(partners):
+                other = spread(ring_ref[row + 1 + down, column + 1 + right])
+                shifted = [own[0] - float(down), own[1] - float(right)] + own[2:]
+                push = pushes(shifted, other, 2.0 * radius)
+                for axis in range(3):
+                    total[axis] = total[axis] + push[axis]
+                    back[3 * index + axis] = back[3 * index + axis] - push[axis]
+            for axis in range(3):
+                if base_ref is not None:
+                    total[axis] = total[axis] + base_ref[cell, axis, pl.ds(start, 8), :]
+                sums_ref[cell, axis, pl.ds(start, 8), :] = total[axis]
+        return tuple(back)
+
+    zeros = tuple(jnp.zeros((8, 128), F32) for _ in range(3 * len(partners)))
+    back = lax.fori_loop(0, 16 // PART, one, zeros)
+    for index, (down, right) in enumerate(partners):
+        lines = [jnp.sum(back[3 * index + axis], axis=0, keepdims=True) for axis in range(3)]
+        partner = (row + down) * 8 + column + right
+        tile = jnp.concatenate(lines + [jnp.zeros((5, 128), F32)], axis=0)
+        out_ref[partner] = out_ref[partner] + tile
+
+
+def inner_pushes(ring_ref, columns_ref, sums_ref, out_ref, base_ref=None):
+    refs = (columns_ref, ring_ref, sums_ref, out_ref, base_ref)
+    out_ref[...] = jnp.zeros_like(out_ref)
+
+    def one(column, carry):
+        own_pushes(0, column, [(1, 0), (0, 1), (1, 1)], *refs)
+        own_pushes(1, column, [(0, 1), (-1, 1)], *refs)
+        return carry
+
+    lax.fori_loop(0, 7, one, 0)
+    own_pushes(0, 7, [(1, 0)], *refs)
+    own_pushes(1, 7, [], *refs)
+
+
+def outer_pushes(ring_ref, columns_ref, sums_ref, out_ref):
     parts = 16 // PART
 
     def one(turn, carry):
-        which, part = lax.div(turn, parts), lax.rem(turn, parts)
-        row, column = lax.div(which, 6), lax.rem(which, 6) + 1
-        blocks = [
-            (other + 1, column + 1 + right, (other - row).astype(F32), float(right))
-            for other in range(2)
-            for right in (-1, 0, 1)
-        ]
-        meet_blocks(row * 8 + column, part, blocks, columns_ref, ring_ref, sums_ref, base_ref)
-        return carry
-
-    lax.fori_loop(0, 12 * parts, one, 0)
-
-
-def outer_pushes(ring_ref, columns_ref, sums_ref, out_ref, base_ref=None):
-    parts = 16 // PART
-
-    def one(turn, carry):
-        which, part = lax.div(turn, parts), lax.rem(turn, parts)
-        row, column = lax.div(which, 6), lax.rem(which, 6) + 1
+        cell, part = lax.div(turn, parts), lax.rem(turn, parts)
+        row, column = lax.div(cell, 8), lax.rem(cell, 8)
         down = (2 * row - 1).astype(F32)
         blocks = [(3 * row, column + 1 + right, down, float(right)) for right in (-1, 0, 1)]
-        meet_blocks(row * 8 + column, part, blocks, columns_ref, ring_ref, sums_ref, sums_ref)
-        return carry
-
-    lax.fori_loop(0, 12 * parts, one, 0)
+        meet_blocks(cell, part, blocks, columns_ref, ring_ref, sums_ref, sums_ref)
+        return carry
+
+    lax.fori_loop(0, 16 * parts, one, 0)
 
     def side(turn, carry):
         which, part = lax.div(turn, parts), lax.rem(turn, parts)
-        row, column = lax.div(which, 2), lax.rem(which, 2) * 7
-        blocks = [
-            (row + 1 + down, column + 1 + right, float(down), float(right))
-            for down in (-1, 0, 1)
-            for right in (-1, 0, 1)
-        ]
-        meet_blocks(row * 8 + column, part, blocks, columns_ref, ring_ref, sums_ref, base_ref)
+        row, end = lax.div(which, 2), lax.rem(which, 2)
+        right = (2 * end - 1).astype(F32)
+        blocks = [(other + 1, 9 * end, (other - row).astype(F32), right) for other in range(2)]
+        meet_blocks(row * 8 + 7 * end, part, blocks, columns_ref, ring_ref, sums_ref, sums_ref)
         return carry
 
     lax.fori_loop(0, 4 * parts, side, 0)
 
     def gather(cell, carry):
-        out_ref[cell] = across_lanes(sums_ref, cell)
+        out_ref[cell] = out_ref[cell] + across_lanes(sums_ref, cell)
         return carry
 
     lax.fori_loop(0, 16, gather, 0, unroll=4)
@@ -309,7 +333,7 @@
         return carry
 
     lax.fori_loop(1, N_PEERS, start, 0)
-    inner_pushes(ring, columns, sums)
+    inner_pushes(ring, columns, sums, push_ref)
     for index in range(8):
         halo_copy(index, ring, halo_out, halo_in).wait()
     clear_edges(ring)
@@ -446,11 +470,11 @@
         return carry
 
     lax.fori_loop(1, N_PEERS, start, 0)
-    inner_pushes(ring, columns, sums, base_ref)
+    inner_pushes(ring, columns, sums, push_ref, base_ref)
     for index in range(8):
         halo_copy(index, ring, halo_out, halo_in).wait()
     clear_edges(ring)
-    outer_pushes(ring, columns, sums, push_ref, base_ref)
+    outer_pushes(ring, columns, sums, push_ref)
     for slot in range(4):
         back_ref[me * 4 + slot] = impulse_ref[me * 4 + slot, 0:3, :]
 

time: 113 us -> 109 us (0.965)
  Pallas kernels: 109 us -> 105 us
    pallas_call x1, Pallas kernels: 54.3 us -> 50.2 us  [body(): pl.pallas_call(second_kernel, out_shape=(tiles, shape((256, 3, 128), F32)...]
where the time goes in v4:
time: 109 us
  Pallas kernels  105 us (96%)
  other arithmetic  2.46 us (2%)
    pallas_call x1, Pallas kernels, body(): pl.pallas_call(second_kernel, out_shape=(tiles, shape((256, 3, 128), F32)...  50.2 us
    pallas_call x1, Pallas kernels, body(): pl.pallas_call(first_kernel, out_shape=(shape((257, 8, 128), F32), shape(...  35.8 us
    pallas_call x1, Pallas kernels, body(): pl.pallas_call(face_kernel, out_shape=(tiles, shape((16, 3, 128, 128), F3...  15.5 us

profile of v4, /device:TPU:1, one launch (start us, length us, event | category | flops | bytes accessed | tf_op | source)
XLA Modules:
  0.0 108.5 jit_solution(12599599484900867956)
XLA Ops:
  0.6 0.8 reshape.13
  1.4 0.7 pad_add_fusion.ints_ref.count_ref
  2.1 0.8 pad_maximum_fusion.1.parts_ref
  2.9 1.0 pad_maximum_fusion.blocks_ref
  3.9 1.7 %pack.1 = (f32[16,8,128]{2,1,0:T(8,128)S(1)}, f32[64,25,128]{2,1,0:T(8,128)S(1)}, s32[64]{0:T(128)S(1)}) custom-call(f32[6,2,8,128]{3,2,1,0:T(8,128)S(1)} %pad_maximum_fusion.1.parts_ref, f32[6,64,128]{2,1,0:T(8,128)S(1)} %pad_maximum_fusion.blocks_ref, s32[144]{0:T(256)S(1)} %pad_add_fusion.ints_ref.count_ref), custom_call_target="tpu_custom_call" | custom-call | tf_op jit(solution)/shard_map/pack/pallas_call | solution.py:527
  5.6 35.8 %exchange_faces.1 = (f32[257,8,128]{2,1,0:T(8,128)S(1)}, f32[64,1,128]{2,1,0:T(1,128)S(1)}, f32[16,8,128]{2,1,0:T(8,128)S(1)}) custom-call(f32[16,8,128]{2,1,0:T(8,128)S(1)} %get-tuple-element.17.state_ref, f32[64,25,128]{2,1,0:T(8,128)S(1)} %get-tuple-element.18.send_ref, s32[144]{0:T(256)S(1)} %pad_add_fusion.ints_ref.count_ref), custom_call_target="tpu_custom_call" | custom-call | tf_op jit(solution)/shard_map/exchange_faces/pallas_call | solution.py:543
  41.4 15.5 %faces.1 = (f32[16,8,128]{2,1,0:T(8,128)S(1)}, f32[16,3,128,128]{3,2,1,0:T(8,128)S(1)}, f32[257,8,128]{2,1,0:T(8,128)S(1)}) custom-call(f32[257,8,128]{2,1,0:T(8,128)S(1)} %get-tuple-element.19.faces_ref, f32[64,1,128]{2,1,0:T(1,128)S(1)} %get-tuple-element.20.cells_ref, f32[16,8,128]{2,1,0:T(8,128)S(1)} %get-tuple-element.17.state_ref, ...), custom_call_target="tpu_custom_call" | custom-call | tf_op jit(solution)/shard_map/faces/pallas_call | solution.py:557
  56.9 50.2 %exchange_impulses.1 = (f32[16,8,128]{2,1,0:T(8,128)S(1)}, f32[256,3,128]{2,1,0:T(4,128)S(1)}) custom-call(f32[16,8,128]{2,1,0:T(8,128)S(1)} %get-tuple-element.22.state_ref, f32[257,8,128]{2,1,0:T(8,128)S(1)} %get-tuple-element.23.impulse_ref, f32[16,3,128,128]{3,2,1,0:T(8,128)S(1)} %get-tuple-element.24.base_ref, s32[144]{0:T(256)S(1)} %pad_add_fusion.ints_ref.count_ref), custom_call_target="tpu_custom_call" | custom-call | tf_op jit(solution)/shard_map/exchange_impulses/pallas_call | solution.py:572
  107.1 1.4 %finish.1 = (f32[3,2,8,128]{3,2,1,0:T(8,128)}, f32[3,2,8,128]{3,2,1,0:T(8,128)}, f32[3,64,128]{2,1,0:T(8,128)}) custom-call(f32[16,8,128]{2,1,0:T(8,128)S(1)} %get-tuple-element.22.state_ref, f32[16,8,128]{2,1,0:T(8,128)S(1)} %get-tuple-element.25.push_ref, s32[144]{0:T(256)S(1)} %pad_add_fusion.ints_ref.count_ref, ...), custom_call_target="tpu_custom_call" | custom-call | tf_op jit(solution)/shard_map/finish/pallas_call | solution.py:587

commit v5 on v4

--- a/solution.py
+++ b/solution.py
@@ -24,7 +24,7 @@
 SIDES = [(a, b) for a in (-1, 0, 1) for b in (-1, 0, 1) if (a, b) != (0, 0)]
 N_PEERS = 64
 COUNTS = 128
-PART = 2
+PART = 4
 WIDTH = 2
 
 
@@ -373,7 +373,7 @@
         filled[cell] = count + 1
         return carry
 
-    lax.fori_loop(0, 256, enter, 0, unroll=4)
+    lax.fori_loop(0, 256, enter, 0, unroll=16)
     for cell in range(16):
         for extra in range(WIDTH - 1):
             listing[cell * room + filled[cell] + extra] = 256

time: 109 us -> 106 us (0.972)
  Pallas kernels: 105 us -> 102 us
    pallas_call x1, Pallas kernels: 50.2 us -> 45.4 us  [body(): pl.pallas_call(second_kernel, out_shape=(tiles, shape((256, 3, 128), F32)...]
    pallas_call x1, Pallas kernels: 15.5 us -> 17.2 us  [body(): pl.pallas_call(face_kernel, out_shape=(tiles, shape((16, 3, 128, 128), F3...]
where the time goes in v5:
time: 106 us
  Pallas kernels  102 us (96%)
  other arithmetic  2.46 us (2%)
    pallas_call x1, Pallas kernels, body(): pl.pallas_call(second_kernel, out_shape=(tiles, shape((256, 3, 128), F32)...  45.4 us
    pallas_call x1, Pallas kernels, body(): pl.pallas_call(first_kernel, out_shape=(shape((257, 8, 128), F32), shape(...  35.8 us
    pallas_call x1, Pallas kernels, body(): pl.pallas_call(face_kernel, out_shape=(tiles, shape((16, 3, 128, 128), F3...  17.2 us

profile of v5, /device:TPU:1, one launch (start us, length us, event | category | flops | bytes accessed | tf_op | source)
XLA Modules:
  0.0 105.5 jit_solution(9329417193003014671)
XLA Ops:
  0.6 0.8 reshape.13
  1.4 0.7 pad_add_fusion.ints_ref.count_ref
  2.1 0.8 pad_maximum_fusion.1.parts_ref
  2.9 1.0 pad_maximum_fusion.blocks_ref
  3.9 1.7 %pack.1 = (f32[16,8,128]{2,1,0:T(8,128)S(1)}, f32[64,25,128]{2,1,0:T(8,128)S(1)}, s32[64]{0:T(128)S(1)}) custom-call(f32[6,2,8,128]{3,2,1,0:T(8,128)S(1)} %pad_maximum_fusion.1.parts_ref, f32[6,64,128]{2,1,0:T(8,128)S(1)} %pad_maximum_fusion.blocks_ref, s32[144]{0:T(256)S(1)} %pad_add_fusion.ints_ref.count_ref), custom_call_target="tpu_custom_call" | custom-call | tf_op jit(solution)/shard_map/pack/pallas_call | solution.py:527
  5.6 35.8 %exchange_faces.1 = (f32[257,8,128]{2,1,0:T(8,128)S(1)}, f32[64,1,128]{2,1,0:T(1,128)S(1)}, f32[16,8,128]{2,1,0:T(8,128)S(1)}) custom-call(f32[16,8,128]{2,1,0:T(8,128)S(1)} %get-tuple-element.17.state_ref, f32[64,25,128]{2,1,0:T(8,128)S(1)} %get-tuple-element.18.send_ref, s32[144]{0:T(256)S(1)} %pad_add_fusion.ints_ref.count_ref), custom_call_target="tpu_custom_call" | custom-call | tf_op jit(solution)/shard_map/exchange_faces/pallas_call | solution.py:543
  41.4 17.2 %faces.1 = (f32[16,8,128]{2,1,0:T(8,128)S(1)}, f32[16,3,128,128]{3,2,1,0:T(8,128)S(1)}, f32[257,8,128]{2,1,0:T(8,128)S(1)}) custom-call(f32[257,8,128]{2,1,0:T(8,128)S(1)} %get-tuple-element.19.faces_ref, f32[64,1,128]{2,1,0:T(1,128)S(1)} %get-tuple-element.20.cells_ref, f32[16,8,128]{2,1,0:T(8,128)S(1)} %get-tuple-element.17.state_ref, ...), custom_call_target="tpu_custom_call" | custom-call | tf_op jit(solution)/shard_map/faces/pallas_call | solution.py:557
  58.6 45.4 %exchange_impulses.1 = (f32[16,8,128]{2,1,0:T(8,128)S(1)}, f32[256,3,128]{2,1,0:T(4,128)S(1)}) custom-call(f32[16,8,128]{2,1,0:T(8,128)S(1)} %get-tuple-element.22.state_ref, f32[257,8,128]{2,1,0:T(8,128)S(1)} %get-tuple-element.23.impulse_ref, f32[16,3,128,128]{3,2,1,0:T(8,128)S(1)} %get-tuple-element.24.base_ref, s32[144]{0:T(256)S(1)} %pad_add_fusion.ints_ref.count_ref), custom_call_target="tpu_custom_call" | custom-call | tf_op jit(solution)/shard_map/exchange_impulses/pallas_call | solution.py:572
  104.1 1.4 %finish.1 = (f32[3,2,8,128]{3,2,1,0:T(8,128)}, f32[3,2,8,128]{3,2,1,0:T(8,128)}, f32[3,64,128]{2,1,0:T(8,128)}) custom-call(f32[16,8,128]{2,1,0:T(8,128)S(1)} %get-tuple-element.22.state_ref, f32[16,8,128]{2,1,0:T(8,128)S(1)} %get-tuple-element.25.push_ref, s32[144]{0:T(256)S(1)} %pad_add_fusion.ints_ref.count_ref, ...), custom_call_target="tpu_custom_call" | custom-call | tf_op jit(solution)/shard_map/finish/pallas_call | solution.py:587

commit v6 on v5

--- a/solution.py
+++ b/solution.py
@@ -103,7 +103,7 @@
 
     for side in SIDES:
         pl.semaphore_signal(barrier, inc=1, device_id=neighbour(side), device_id_type=MESH)
-    lax.fori_loop(1, N_PEERS, one, 0)
+    lax.fori_loop(1, N_PEERS, one, 0, unroll=3)
 
 
 def meet_all():
@@ -280,7 +280,7 @@
         out_ref[cell] = out_ref[cell] + across_lanes(sums_ref, cell)
         return carry
 
-    lax.fori_loop(0, 16, gather, 0, unroll=4)
+    lax.fori_loop(0, 16, gather, 0, unroll=8)
 
 
 def pack_kernel(parts_ref, blocks_ref, ints_ref, state_ref, send_ref, pos_ref, used):
@@ -332,7 +332,7 @@
         block_copy(step, send_ref, recv, data_out, data_in).start()
         return carry
 
-    lax.fori_loop(1, N_PEERS, start, 0)
+    lax.fori_loop(1, N_PEERS, start, 0, unroll=3)
     inner_pushes(ring, columns, sums, push_ref)
     for index in range(8):
         halo_copy(index, ring, halo_out, halo_in).wait()
@@ -353,7 +353,7 @@
         cells_ref[source] = recv[source, 24:25, :]
         return carry
 
-    lax.fori_loop(1, N_PEERS, finish, 0)
+    lax.fori_loop(1, N_PEERS, finish, 0, unroll=3)
 
 
 def face_kernel(
@@ -431,7 +431,7 @@
                 next_ref[cell] = tile
                 return carry
 
-            lax.fori_loop(0, 16, advance, 0, unroll=4)
+            lax.fori_loop(0, 16, advance, 0, unroll=8)
 
         return carry
 
@@ -469,7 +469,7 @@
         block_copy(step, outgoing, recv, data_out, data_in).start()
         return carry
 
-    lax.fori_loop(1, N_PEERS, start, 0)
+    lax.fori_loop(1, N_PEERS, start, 0, unroll=3)
     inner_pushes(ring, columns, sums, push_ref, base_ref)
     for index in range(8):
         halo_copy(index, ring, halo_out, halo_in).wait()
@@ -487,7 +487,7 @@
             back_ref[source * 4 + slot] = recv[source, slot * 3 : slot * 3 + 3, :]
         return carry
 
-    lax.fori_loop(1, N_PEERS, finish, 0)
+    lax.fori_loop(1, N_PEERS, finish, 0, unroll=3)
 
 
 def last_kernel(state_ref, push_ref, count_ref, back_ref, pos_ref, offset_ref, velocity_ref, impulse_ref):

time: 106 us -> 106 us (level)
  the two profiles are of different devices: /device:TPU:1 before, /device:TPU:22 now
where the time goes in v6:
time: 106 us
  Pallas kernels  102 us (96%)
  other arithmetic  2.46 us (2%)
    pallas_call x1, Pallas kernels, body(): pl.pallas_call(second_kernel, out_shape=(tiles, shape((256, 3, 128), F32)...  49.8 us
    pallas_call x1, Pallas kernels, body(): pl.pallas_call(first_kernel, out_shape=(shape((257, 8, 128), F32), shape(...  33 us
    pallas_call x1, Pallas kernels, body(): pl.pallas_call(face_kernel, out_shape=(tiles, shape((16, 3, 128, 128), F3...  16.2 us

profile of v6, /device:TPU:22, one launch (start us, length us, event | category | flops | bytes accessed | tf_op | source)
XLA Modules:
  0.0 105.9 jit_solution(11245167543966428871)
XLA Ops:
  0.6 0.8 reshape.13
  1.4 0.7 pad_add_fusion.ints_ref.count_ref
  2.1 0.8 pad_maximum_fusion.1.parts_ref
  2.9 1.0 pad_maximum_fusion.blocks_ref
  3.9 1.7 %pack.1 = (f32[16,8,128]{2,1,0:T(8,128)S(1)}, f32[64,25,128]{2,1,0:T(8,128)S(1)}, s32[64]{0:T(128)S(1)}) custom-call(f32[6,2,8,128]{3,2,1,0:T(8,128)S(1)} %pad_maximum_fusion.1.parts_ref, f32[6,64,128]{2,1,0:T(8,128)S(1)} %pad_maximum_fusion.blocks_ref, s32[144]{0:T(256)S(1)} %pad_add_fusion.ints_ref.count_ref), custom_call_target="tpu_custom_call" | custom-call | tf_op jit(solution)/shard_map/pack/pallas_call | solution.py:527
  5.6 33.0 %exchange_faces.1 = (f32[257,8,128]{2,1,0:T(8,128)S(1)}, f32[64,1,128]{2,1,0:T(1,128)S(1)}, f32[16,8,128]{2,1,0:T(8,128)S(1)}) custom-call(f32[16,8,128]{2,1,0:T(8,128)S(1)} %get-tuple-element.17.state_ref, f32[64,25,128]{2,1,0:T(8,128)S(1)} %get-tuple-element.18.send_ref, s32[144]{0:T(256)S(1)} %pad_add_fusion.ints_ref.count_ref), custom_call_target="tpu_custom_call" | custom-call | tf_op jit(solution)/shard_map/exchange_faces/pallas_call | solution.py:543
  38.6 16.2 %faces.1 = (f32[16,8,128]{2,1,0:T(8,128)S(1)}, f32[16,3,128,128]{3,2,1,0:T(8,128)S(1)}, f32[257,8,128]{2,1,0:T(8,128)S(1)}) custom-call(f32[257,8,128]{2,1,0:T(8,128)S(1)} %get-tuple-element.19.faces_ref, f32[64,1,128]{2,1,0:T(1,128)S(1)} %get-tuple-element.20.cells_ref, f32[16,8,128]{2,1,0:T(8,128)S(1)} %get-tuple-element.17.state_ref, ...), custom_call_target="tpu_custom_call" | custom-call | tf_op jit(solution)/shard_map/faces/pallas_call | solution.py:557
  54.7 49.8 %exchange_impulses.1 = (f32[16,8,128]{2,1,0:T(8,128)S(1)}, f32[256,3,128]{2,1,0:T(4,128)S(1)}) custom-call(f32[16,8,128]{2,1,0:T(8,128)S(1)} %get-tuple-element.22.state_ref, f32[257,8,128]{2,1,0:T(8,128)S(1)} %get-tuple-element.23.impulse_ref, f32[16,3,128,128]{3,2,1,0:T(8,128)S(1)} %get-tuple-element.24.base_ref, s32[144]{0:T(256)S(1)} %pad_add_fusion.ints_ref.count_ref), custom_call_target="tpu_custom_call" | custom-call | tf_op jit(solution)/shard_map/exchange_impulses/pallas_call | solution.py:572
  104.5 1.4 %finish.1 = (f32[3,2,8,128]{3,2,1,0:T(8,128)}, f32[3,2,8,128]{3,2,1,0:T(8,128)}, f32[3,64,128]{2,1,0:T(8,128)}) custom-call(f32[16,8,128]{2,1,0:T(8,128)S(1)} %get-tuple-element.22.state_ref, f32[16,8,128]{2,1,0:T(8,128)S(1)} %get-tuple-element.25.push_ref, s32[144]{0:T(256)S(1)} %pad_add_fusion.ints_ref.count_ref, ...), custom_call_target="tpu_custom_call" | custom-call | tf_op jit(solution)/shard_map/finish/pallas_call | solution.py:587
